TPU v7x, 32 devices: a whole 2x2x4 slice. The times are simulated.
32 devices in a mesh: tm: 16 (over z, y, x), ffn: 2 (over core).
Axes of the slice: x: 2, y: 2, z: 4, core: 2. Of those that a mesh axis runs over, the one named last changes fastest.
Arguments:
- frames: bfloat16 [32768, 512], P('tm'), may hold values from -60 to 60
- upstream: bfloat16 [32768, 512], P('tm'), may hold values from -6 to 6
- recording: int32 [32768], replicated, may hold values from 0 to 3, never falling along the last dimension, each value on 1 to 16384 neighbouring positions
- first_gain: float32 [512], replicated, may hold values from 0.1 to 1.9
- query_weight: bfloat16 [512, 512], P(None, 'ffn'), may hold values from -0.5 to 0.5
- key_weight: bfloat16 [512, 512], P(None, 'ffn'), may hold values from -0.5 to 0.5
- value_weight: bfloat16 [512, 512], P(None, 'ffn'), may hold values from -0.25 to 0.25
- out_weight: bfloat16 [512, 512], P('ffn'), may hold values from -0.25 to 0.25
- second_gain: float32 [512], replicated, may hold values from 0.1 to 1.9
- inner_weight: bfloat16 [512, 2048], P(None, 'ffn'), may hold values from -0.25 to 0.25
- outer_weight: bfloat16 [2048, 512], P('ffn'), may hold values from -0.125 to 0.125
Outputs:
- grad_frames: float32 [32768, 512], P(('tm', 'ffn'))
- grad_query_weight: float32 [512, 512], P(None, 'ffn')
- grad_key_weight: float32 [512, 512], P(None, 'ffn')
- grad_value_weight: float32 [512, 512], P(None, 'ffn')
- grad_out_weight: float32 [512, 512], P('ffn')
- grad_inner_weight: float32 [512, 2048], P(None, 'ffn')
- grad_outer_weight: float32 [2048, 512], P('ffn')
Inputs may be any that keep to these rules, and one draw needn't show every extreme that they name: Ids never fall along time; each recording spans 1 to 16384 frames and one spans exactly that many.
All inputs are finite; a program needn't handle non-finite values.
Results may differ from a plain program's by a relative error of at most 0.025.
Values may be sent and summed in bfloat16 or wider, within the bound.
A program may use at most 128 MiB of HBM per device.

v0:
```python
import math

import jax
import jax.numpy as jnp
from jax import lax
from jax.sharding import PartitionSpec as P

HEAD_DIM = 64
HALF = 256


epsilon = 1e-05
masked_score = -1e30


def with_halo(cells, sides, width):
    for axis, dim in sides:
        count = lax.axis_size(axis)
        ends = count - 1
        head = lax.slice_in_dim(cells, 0, width, axis=dim)
        tail = lax.slice_in_dim(cells, cells.shape[dim] - width, cells.shape[dim], axis=dim)
        cells = jnp.concatenate(
            [
                lax.ppermute(tail, axis, [(i, (i + 1) % count) for i in range(ends)]),
                cells,
                lax.ppermute(head, axis, [((i + 1) % count, i) for i in range(ends)]),
            ],
            axis=dim,
        )
    return cells


def layer_norm(inputs):
    center = jnp.mean(inputs, axis=-1, keepdims=True)
    shifted = inputs - center
    inverse = lax.rsqrt(jnp.mean(shifted * shifted, axis=-1, keepdims=True) + epsilon)
    return (shifted * inverse, inverse)


def norm_back(grad_normed, scaled, inverse, gain):
    weighted = grad_normed * gain
    first_mean = jnp.mean(weighted, axis=-1, keepdims=True)
    second_mean = jnp.mean(weighted * scaled, axis=-1, keepdims=True)
    return inverse * (weighted - first_mean - scaled * second_mean)


def project(normed, weight):
    return jnp.dot(normed, weight, preferred_element_type=jnp.float32).astype(jnp.bfloat16)


def block_allowed(record_query, record_key):
    block_rows = record_query.shape[0]
    offsets = lax.broadcasted_iota(
        jnp.int32, (block_rows, 2 * block_rows), 1
    ) - lax.broadcasted_iota(jnp.int32, (block_rows, 2 * block_rows), 0)
    band = (offsets >= 0) & (offsets < block_rows)
    return band & (record_query[:, None] == record_key[None, :])


def masked_scores(query_block, key_block, allowed):
    scores = jnp.einsum(
        "qhd,khd->hqk", query_block, key_block, preferred_element_type=jnp.float32
    ) * HEAD_DIM ** (-0.5)
    return jnp.where(allowed[None], scores, masked_score)


def tile_scores(query_block, key_block, allowed):
    return masked_scores(query_block, key_block, allowed)


def softmax_rows(scores):
    peak = jnp.max(scores, axis=-1, keepdims=True)
    weights = jnp.exp(scores - peak)
    return weights / jnp.sum(weights, axis=-1, keepdims=True)


def score_grads(grad_block, value_tile):
    return jnp.einsum("qhd,khd->hqk", grad_block, value_tile, preferred_element_type=jnp.float32)


def query_grads(score_tile, key_tile):
    return jnp.einsum("hqk,khd->qhd", score_tile, key_tile, preferred_element_type=jnp.float32)


def key_grads(score_tile, query_block):
    return jnp.einsum("hqk,qhd->khd", score_tile, query_block, preferred_element_type=jnp.float32)


def block_context(query_block, key_block, value_block, allowed):
    probability = softmax_rows(tile_scores(query_block, key_block, allowed))
    context = jnp.einsum(
        "hqk,khd->qhd",
        probability.astype(jnp.bfloat16),
        value_block,
        preferred_element_type=jnp.float32,
    )
    return context.astype(jnp.bfloat16)


def block_backward(query_block, key_block, value_block, grad_block, allowed):
    probability = softmax_rows(tile_scores(query_block, key_block, allowed))
    probability_low = probability.astype(jnp.bfloat16)
    grad_prob = score_grads(grad_block, value_block)
    inner_sum = jnp.sum(grad_prob * probability, axis=-1, keepdims=True)
    grad_scores = (probability * (grad_prob - inner_sum) * HEAD_DIM ** (-0.5)).astype(jnp.bfloat16)
    grad_query = query_grads(grad_scores, key_block)
    grad_key = key_grads(grad_scores, query_block)
    grad_value = key_grads(probability_low, grad_block)
    return (grad_query, grad_key, grad_value)


def local(
    frames,
    upstream,
    recording,
    first_gain,
    query_weight,
    key_weight,
    value_weight,
    out_weight,
    second_gain,
    inner_weight,
    outer_weight,
):
    slab_rows = frames.shape[0]
    block_rows = 2 * HALF
    head_cols = query_weight.shape[1]
    local_heads = head_cols // HEAD_DIM
    share_rows = slab_rows // lax.axis_size("ffn")
    share_start = lax.axis_index("ffn") * share_rows
    record_pad = jnp.pad(recording, (HALF, HALF), constant_values=-1)
    record_ext = lax.dynamic_slice_in_dim(
        record_pad, lax.axis_index("tm") * slab_rows, slab_rows + 2 * HALF
    )
    frames_wide = frames.astype(jnp.float32)
    upstream_wide = upstream.astype(jnp.float32)
    scaled_first, inverse_first = layer_norm(frames_wide)
    normed_first = (scaled_first * first_gain).astype(jnp.bfloat16)
    queries = project(normed_first, query_weight)
    key_rows = project(normed_first, key_weight)
    value_rows = project(normed_first, value_weight)
    key_value = jnp.concatenate([key_rows, value_rows], axis=1)
    key_value_ext = with_halo(key_value, (("tm", 0),), HALF)
    blocks = slab_rows // block_rows
    pieces = []
    contexts = []
    for block_index in range(blocks):
        first_row = block_index * block_rows
        query_block = queries[first_row : first_row + block_rows].reshape(
            block_rows, local_heads, HEAD_DIM
        )
        ext_block = key_value_ext[first_row : first_row + 2 * block_rows]
        key_block = ext_block[:, :head_cols].reshape(2 * block_rows, local_heads, HEAD_DIM)
        value_block = ext_block[:, head_cols:].reshape(2 * block_rows, local_heads, HEAD_DIM)
        allowed = block_allowed(
            record_ext[HALF + first_row : HALF + first_row + block_rows],
            record_ext[first_row : first_row + 2 * block_rows],
        )
        pieces.append((query_block, key_block, value_block, allowed))
        contexts.append(
            block_context(query_block, key_block, value_block, allowed).reshape(
                block_rows, head_cols
            )
        )
    context = jnp.concatenate(contexts, axis=0)
    partial_value = jnp.dot(context, out_weight, preferred_element_type=jnp.float32)
    middle = frames_wide + lax.psum(partial_value.astype(jnp.bfloat16), "ffn").astype(jnp.float32)
    scaled_second, inverse_second = layer_norm(middle)
    normed_second = (scaled_second * second_gain).astype(jnp.bfloat16)
    inner_pre = jnp.dot(normed_second, inner_weight, preferred_element_type=jnp.float32)
    activation = jax.nn.silu(inner_pre).astype(jnp.bfloat16)
    sigmoid_inner = jax.nn.sigmoid(inner_pre)
    grad_act = jnp.dot(upstream, outer_weight.T, preferred_element_type=jnp.float32) * 0.5
    grad_inner = (grad_act * sigmoid_inner * (1.0 + inner_pre * (1.0 - sigmoid_inner))).astype(
        jnp.bfloat16
    )
    grad_outer_terms = jnp.dot(activation.T, upstream, preferred_element_type=jnp.float32) * 0.5
    grad_inner_terms = jnp.dot(normed_second.T, grad_inner, preferred_element_type=jnp.float32)
    grad_second_part = jnp.dot(grad_inner, inner_weight.T, preferred_element_type=jnp.float32)
    grad_second = lax.psum(grad_second_part.astype(jnp.bfloat16), "ffn").astype(jnp.float32)
    grad_middle = upstream_wide + norm_back(grad_second, scaled_second, inverse_second, second_gain)
    grad_middle_low = grad_middle.astype(jnp.bfloat16)
    grad_middle_share = lax.dynamic_slice_in_dim(grad_middle, share_start, share_rows, 0)
    grad_out_terms = jnp.dot(context.T, grad_middle_low, preferred_element_type=jnp.float32)
    grad_context = jnp.dot(
        grad_middle_low, out_weight.T, preferred_element_type=jnp.float32
    ).astype(jnp.bfloat16)
    grad_pairs_ext = jnp.zeros((slab_rows + 2 * HALF, 2 * head_cols), jnp.float32)
    query_parts = []
    for block_index, (query_block, key_block, value_block, allowed) in enumerate(pieces):
        first_row = block_index * block_rows
        grad_block = grad_context[first_row : first_row + block_rows].reshape(
            block_rows, local_heads, HEAD_DIM
        )
        grad_query, grad_key, grad_value = block_backward(
            query_block, key_block, value_block, grad_block, allowed
        )
        query_parts.append(grad_query.reshape(block_rows, head_cols))
        grad_pair = jnp.concatenate(
            [
                grad_key.reshape(2 * block_rows, head_cols),
                grad_value.reshape(2 * block_rows, head_cols),
            ],
            axis=1,
        )
        grad_pairs_ext = grad_pairs_ext.at[first_row : first_row + 2 * block_rows].add(grad_pair)
    outer_rims = jnp.concatenate(
        [grad_pairs_ext[:HALF], grad_pairs_ext[slab_rows + HALF :]], axis=0
    )
    received = with_halo(outer_rims.astype(jnp.bfloat16), (("tm", 0),), HALF).astype(
        outer_rims.dtype
    )
    from_lower = received[:HALF]
    from_upper = received[3 * HALF :]
    grad_pairs = grad_pairs_ext[HALF : HALF + slab_rows]
    grad_pairs = (
        grad_pairs
        + jnp.pad(from_lower, ((0, slab_rows - HALF), (0, 0)))
        + jnp.pad(from_upper, ((slab_rows - HALF, 0), (0, 0)))
    )
    grad_query_low = jnp.concatenate(query_parts, axis=0).astype(jnp.bfloat16)
    grad_key_low = grad_pairs[:, :head_cols].astype(jnp.bfloat16)
    grad_value_low = grad_pairs[:, head_cols:].astype(jnp.bfloat16)
    grad_query_terms = jnp.dot(normed_first.T, grad_query_low, preferred_element_type=jnp.float32)
    grad_key_terms = jnp.dot(normed_first.T, grad_key_low, preferred_element_type=jnp.float32)
    grad_value_terms = jnp.dot(normed_first.T, grad_value_low, preferred_element_type=jnp.float32)
    grad_first_part = jnp.dot(grad_query_low, query_weight.T, preferred_element_type=jnp.float32)
    grad_first_part = grad_first_part + jnp.dot(
        grad_key_low, key_weight.T, preferred_element_type=jnp.float32
    )
    grad_first_part = grad_first_part + jnp.dot(
        grad_value_low, value_weight.T, preferred_element_type=jnp.float32
    )
    grad_first_share = lax.psum_scatter(
        grad_first_part.astype(jnp.bfloat16), "ffn", scatter_dimension=0, tiled=True
    ).astype(jnp.float32)
    scaled_share = lax.dynamic_slice_in_dim(scaled_first, share_start, share_rows, 0)
    inverse_share = lax.dynamic_slice_in_dim(inverse_first, share_start, share_rows, 0)
    grad_frames = grad_middle_share + norm_back(
        grad_first_share, scaled_share, inverse_share, first_gain
    )
    weight_scale = 1.0 / math.sqrt(recording.shape[0])
    totals = (
        lax.psum(grad_query_terms.astype(jnp.bfloat16), "tm").astype(jnp.float32),
        lax.psum(grad_key_terms.astype(jnp.bfloat16), "tm").astype(jnp.float32),
        lax.psum(grad_value_terms.astype(jnp.bfloat16), "tm").astype(jnp.float32),
        lax.psum(grad_out_terms.astype(jnp.bfloat16), "tm").astype(jnp.float32),
        lax.psum(grad_inner_terms.astype(jnp.bfloat16), "tm").astype(jnp.float32),
        lax.psum(grad_outer_terms.astype(jnp.bfloat16), "tm").astype(jnp.float32),
    )
    return (grad_frames,) + tuple((total * weight_scale for total in totals))


def solution(mesh):
    in_specs = (
        P("tm", None),
        P("tm", None),
        P(),
        P(),
        P(None, "ffn"),
        P(None, "ffn"),
        P(None, "ffn"),
        P("ffn", None),
        P(),
        P(None, "ffn"),
        P("ffn", None),
    )
    out_specs = (
        P(("tm", "ffn"), None),
        P(None, "ffn"),
        P(None, "ffn"),
        P(None, "ffn"),
        P("ffn", None),
        P(None, "ffn"),
        P("ffn", None),
    )
    return jax.shard_map(local, mesh=mesh, in_specs=in_specs, out_specs=out_specs, check_vma=False)
```

profile of v0, /device:TPU:0, one launch (start us, length us, event | category | flops | bytes accessed | tf_op | source)
XLA Modules:
  0.0 560.0 jit_solution(10052441508470068500)
XLA Ops:
  16.8 5.6 collective-permute-start
  38.3 7.5 %fusion.168 = (f32[4,512]{1,0:T(4,128)S(1)}, f32[4,512,1024]{2,1,0:T(8,128)}) fusion(pred[512,1024]{1,0:T(8,128)(4,1)} %get-tuple-element.110, bf16[512,4,64]{0,2,1:T(8,128)(2,1)} %bitcast.159, bf16[1024,4,64]{0,2,1:T(8,128)(2,1)} %bitcast.151), kind=kOutput, calls=%fused_computation.222 | convolution fusion | flops 276825088 | bytes 9707520 | tf_op jit(solution)/shard_map/sub | solution.py:73
  45.7 5.7 %fusion.92 = bf16[4,64,512]{2,1,0:T(8,128)(2,1)} fusion(bf16[1024,4,64]{0,2,1:T(8,128)(2,1)} %bitcast.127, f32[4,512,1024]{2,1,0:T(8,128)} %get-tuple-element.106, f32[4,512]{1,0:T(4,128)S(1)} %get-tuple-element.105), kind=kOutput, calls=%fused_computation.125 | convolution fusion | flops 272760832 | bytes 9183232 | tf_op jit(solution)/shard_map/hqk,khd->qhd/dot_general | solution.py:91
  51.5 7.4 %fusion.165 = (f32[4,512]{1,0:T(4,128)S(1)}, f32[4,512,1024]{2,1,0:T(8,128)}) fusion(pred[512,1024]{1,0:T(8,128)(4,1)} %get-tuple-element.107, bf16[512,4,64]{0,2,1:T(8,128)(2,1)S(1)} %bitcast.157, bf16[1024,4,64]{0,2,1:T(8,128)(2,1)} %bitcast.149), kind=kOutput, calls=%fused_computation.219 | convolution fusion | flops 276825088 | bytes 9707520 | tf_op jit(solution)/shard_map/sub | solution.py:73
  58.9 5.8 %fusion.101 = bf16[4,64,512]{2,1,0:T(8,128)(2,1)} fusion(bf16[1024,4,64]{0,2,1:T(8,128)(2,1)} %bitcast.125, f32[4,512,1024]{2,1,0:T(8,128)} %get-tuple-element.100, f32[4,512]{1,0:T(4,128)S(1)} %get-tuple-element.99), kind=kOutput, calls=%fused_computation.128 | convolution fusion | flops 272760832 | bytes 9183232 | tf_op jit(solution)/shard_map/hqk,khd->qhd/dot_general | solution.py:91
  64.7 7.8 %fusion.166 = (f32[4,512]{1,0:T(4,128)S(1)}, f32[4,512,1024]{2,1,0:T(8,128)}) fusion(pred[512,1024]{1,0:T(8,128)(4,1)} %get-tuple-element.108, bf16[512,4,64]{0,2,1:T(8,128)(2,1)S(1)} %bitcast.161, bf16[1024,4,64]{0,2,1:T(8,128)(2,1)} %bitcast.153), kind=kOutput, calls=%fused_computation.220 | convolution fusion | flops 276825088 | bytes 9707520 | tf_op jit(solution)/shard_map/sub | solution.py:73
  72.5 5.8 %fusion.98 = bf16[4,64,512]{2,1,0:T(8,128)(2,1)} fusion(bf16[1024,4,64]{0,2,1:T(8,128)(2,1)} %bitcast.129, f32[4,512,1024]{2,1,0:T(8,128)} %get-tuple-element.102, f32[4,512]{1,0:T(4,128)S(1)} %get-tuple-element.101), kind=kOutput, calls=%fused_computation.127 | convolution fusion | flops 272760832 | bytes 9183232 | tf_op jit(solution)/shard_map/hqk,khd->qhd/dot_general | solution.py:91
  78.3 7.4 %fusion.167 = (f32[4,512]{1,0:T(4,128)S(1)}, f32[4,512,1024]{2,1,0:T(8,128)}) fusion(pred[512,1024]{1,0:T(8,128)(4,1)} %get-tuple-element.109, bf16[512,4,64]{0,2,1:T(8,128)(2,1)S(1)} %bitcast.163, bf16[1024,4,64]{0,2,1:T(8,128)(2,1)} %bitcast.155), kind=kOutput, calls=%fused_computation.221 | convolution fusion | flops 276825088 | bytes 9707520 | tf_op jit(solution)/shard_map/sub | solution.py:73
  85.8 5.1 fusion.95
  93.9 21.5 %all-reduce.9.cloned.1.call-done = bf16[2048,512]{1,0:T(8,128)(2,1)} async-done(((bf16[2048,512]{1,0:T(8,128)(2,1)}), bf16[2048,512]{1,0:T(8,128)(2,1)}) %all-reduce.9.cloned.1.call-update) | async-done | bytes 2097168 | tf_op jit(solution)/shard_map/psum | solution.py:167
  121.6 5.3 multiply_convert_fusion.5
  132.7 6.5 %convolution_convert_fusion.6 = bf16[512,1024]{1,0:T(8,128)(2,1)} fusion(bf16[2048,1024]{1,0:T(8,128)(2,1)} %copy-done.67, bf16[2048,512]{1,0:T(8,128)(2,1)} %all-reduce.9.cloned.1.call-done, bf16[2048,512]{1,0:T(8,128)(2,1)S(1)} %copy-done.2, f32[512]{0:T(512)S(1)} %copy-done.55, f32[2048]{0:T(1024)S(1)} %add_rsqrt_fusion, ...), kind=kOutput, calls=%fused_computation.124 | convolution fusion | flops 2155347968 | bytes 9455616 | tf_op jit(solution)/shard_map/dot_general | solution.py:178
  142.6 12.7 %all-reduce.11.cloned.1.call-done = bf16[2048,512]{1,0:T(8,128)(2,1)} async-done(((bf16[2048,512]{1,0:T(8,128)(2,1)}), bf16[2048,512]{1,0:T(8,128)(2,1)}) %all-reduce.11.cloned.1.call-update) | async-done | bytes 2097168 | tf_op jit(solution)/shard_map/psum | solution.py:180
  167.7 4.5 fusion.170
  172.3 22.1 %fusion.110 = bf16[4,64,512]{2,1,0:T(8,128)(2,1)} fusion(bf16[1024,4,64]{0,2,1:T(8,128)(2,1)S(1)} %bitcast.156, f32[4,512,1024]{2,1,0:T(8,128)} %fusion.170, f32[4,512,1024]{2,1,0:T(8,128)} %get-tuple-element.104, f32[4,512]{1,0:T(4,128)S(1)} %get-tuple-element.103), kind=kOutput, calls=%fused_computation.131 | convolution fusion | flops 283249664 | bytes 17571840 | tf_op jit(solution)/shard_map/hqk,khd->qhd/dot_general | solution.py:82
  194.4 18.3 %fusion.50 = f32[4,64,1024]{2,1,0:T(8,128)} fusion(bf16[512,4,64]{0,2,1:T(8,128)(2,1)S(1)} %bitcast.164, f32[4,512,1024]{2,1,0:T(8,128)} %fusion.170, f32[4,512,1024]{2,1,0:T(8,128)} %get-tuple-element.104, f32[4,512]{1,0:T(4,128)S(1)} %get-tuple-element.103), kind=kOutput, calls=%fused_computation.73 | convolution fusion | flops 283118592 | bytes 18096128 | tf_op jit(solution)/shard_map/hqk,qhd->khd/dot_general | solution.py:86
  212.7 5.3 fusion.77
  218.1 4.5 fusion.171
  222.6 21.9 %fusion.107 = bf16[4,64,512]{2,1,0:T(8,128)(2,1)} fusion(bf16[1024,4,64]{0,2,1:T(8,128)(2,1)S(1)} %bitcast.154, f32[4,512,1024]{2,1,0:T(8,128)} %fusion.171, f32[4,512,1024]{2,1,0:T(8,128)} %get-tuple-element.102, f32[4,512]{1,0:T(4,128)S(1)} %get-tuple-element.101), kind=kOutput, calls=%fused_computation.130 | convolution fusion | flops 283249664 | bytes 17571840 | tf_op jit(solution)/shard_map/hqk,khd->qhd/dot_general | solution.py:82
  244.5 18.5 %fusion.56 = f32[4,64,1024]{2,1,0:T(8,128)} fusion(bf16[512,4,64]{0,2,1:T(8,128)(2,1)S(1)} %bitcast.162, f32[4,512,1024]{2,1,0:T(8,128)} %fusion.171, f32[4,512,1024]{2,1,0:T(8,128)} %get-tuple-element.102, f32[4,512]{1,0:T(4,128)S(1)} %get-tuple-element.101), kind=kOutput, calls=%fused_computation.75 | convolution fusion | flops 283118592 | bytes 18096128 | tf_op jit(solution)/shard_map/hqk,qhd->khd/dot_general | solution.py:86
  263.0 4.4 fusion.85
  267.4 4.6 fusion.169
  272.0 21.9 %fusion.113 = bf16[4,64,512]{2,1,0:T(8,128)(2,1)} fusion(bf16[1024,4,64]{0,2,1:T(8,128)(2,1)S(1)} %bitcast.152, f32[4,512,1024]{2,1,0:T(8,128)} %fusion.169, f32[4,512,1024]{2,1,0:T(8,128)} %get-tuple-element.106, f32[4,512]{1,0:T(4,128)S(1)} %copy-done.71), kind=kOutput, calls=%fused_computation.132 | convolution fusion | flops 283249664 | bytes 17571840 | tf_op jit(solution)/shard_map/hqk,khd->qhd/dot_general | solution.py:82
  293.9 18.3 %fusion.44 = f32[4,64,1024]{2,1,0:T(8,128)} fusion(bf16[512,4,64]{0,2,1:T(8,128)(2,1)S(1)} %bitcast.160, f32[4,512,1024]{2,1,0:T(8,128)} %fusion.169, f32[4,512,1024]{2,1,0:T(8,128)} %get-tuple-element.106, f32[4,512]{1,0:T(4,128)S(1)} %copy-done.71), kind=kOutput, calls=%fused_computation.71 | convolution fusion | flops 283118592 | bytes 18096128 | tf_op jit(solution)/shard_map/hqk,qhd->khd/dot_general | solution.py:86
  312.2 4.4 fusion.73
  316.6 4.5 fusion.172
  321.1 21.9 %fusion.104 = bf16[4,64,512]{2,1,0:T(8,128)(2,1)} fusion(bf16[1024,4,64]{0,2,1:T(8,128)(2,1)S(1)} %bitcast.150, f32[4,512,1024]{2,1,0:T(8,128)} %fusion.172, f32[4,512,1024]{2,1,0:T(8,128)} %get-tuple-element.100, f32[4,512]{1,0:T(4,128)S(1)} %copy-done.69), kind=kOutput, calls=%fused_computation.129 | convolution fusion | flops 283249664 | bytes 17571840 | tf_op jit(solution)/shard_map/hqk,khd->qhd/dot_general | solution.py:82
  343.0 18.6 %fusion.62 = f32[4,64,1024]{2,1,0:T(8,128)} fusion(bf16[512,4,64]{0,2,1:T(8,128)(2,1)S(1)} %bitcast.158, f32[4,512,1024]{2,1,0:T(8,128)} %fusion.172, f32[4,512,1024]{2,1,0:T(8,128)} %get-tuple-element.100, f32[4,512]{1,0:T(4,128)S(1)} %copy-done.69), kind=kOutput, calls=%fused_computation.77 | convolution fusion | flops 283118592 | bytes 18096128 | tf_op jit(solution)/shard_map/hqk,qhd->khd/dot_general | solution.py:86
  367.3 4.6 collective-permute-start.2
  377.1 6.0 %collective-permute-done.2 = bf16[256,512]{0,1:T(8,128)(2,1)S(1)} collective-permute-done((bf16[256,512]{0,1:T(8,128)(2,1)S(1)}, bf16[256,512]{0,1:T(8,128)(2,1)S(1)}, u32[]{:S(2)}, u32[]{:S(2)}) %collective-permute-start.2) | collective-permute-done | bytes 262176 | tf_op jit(solution)/shard_map/ppermute | solution.py:24
  391.4 143.1 %all-reduce.13.cloned.1.call-done = (bf16[512,256]{1,0:T(8,128)(2,1)}, bf16[512,256]{1,0:T(8,128)(2,1)}, bf16[512,256]{1,0:T(8,128)(2,1)}, bf16[256,512]{1,0:T(8...) async-done(((bf16[512,256]{1,0:T(8,128)(2,1)}, bf16[512,256]{1,0:T(8,128)(2,1)}, bf16[512,256]{1,0:T(8,128)(2,1)}, bf16[256,512]{1,0:T(8,128)(2,1)}, ...) | async-done | bytes 3145744 | tf_op jit(solution)/shard_map/psum | solution.py:244
  548.8 4.4 multiply_add_fusion.1
  (219 shorter events, 89.3 us)
Async XLA Ops:
  7.2 111.6 %copy-start = (bf16[512,1024]{1,0:T(8,128)(2,1)S(1)}, bf16[512,1024]{1,0:T(8,128)(2,1)}, u32[]{:S(2)}) copy-start(bf16[512,1024]{1,0:T(8,128)(2,1)} %param.28) | copy-start | bytes 3145732
  7.2 108.2 %all-reduce.9.cloned.1.call-start = ((), (), s32[]{:S(2)}) async-start(), calls=%async_computation.1 | async-start | bytes 4194304 | tf_op jit(solution)/shard_map/psum | solution.py:167
  14.3 9.6 %copy-start.37 = (s32[32768]{0:T(1024)S(1)}, s32[32768]{0:T(1024)}, u32[]{:S(2)}) copy-start(s32[32768]{0:T(1024)} %param.21) | copy-start | bytes 393220
  15.1 12.3 %copy-start.31 = (bf16[512,256]{1,0:T(8,128)(2,1)S(1)}, bf16[512,256]{1,0:T(8,128)(2,1)}, u32[]{:S(2)}) copy-start(bf16[512,256]{1,0:T(8,128)(2,1)} %param.23) | copy-start | bytes 786436
  15.9 6.5 %copy-start.10 = (bf16[2048,256]{0,1:T(8,128)(2,1)}, bf16[2048,256]{0,1:T(8,128)(2,1)S(1)}, u32[]{:S(2)}) copy-start(bf16[2048,256]{0,1:T(8,128)(2,1)S(1)} %convolution_convert_fusion.5) | copy-start | bytes 3145732
  16.8 16.4 %collective-permute-start = (bf16[256,512]{0,1:T(8,128)(2,1)}, bf16[256,512]{0,1:T(8,128)(2,1)}, u32[]{:S(2)}, u32[]{:S(2)}) collective-permute-start(bf16[256,512]{0,1:T(8,128)(2,1)} %get-tuple-element.75), channel_id=1, source_target_pairs={{0,2},{2,4},{4,6},{6,8},{8,10},{10,12},{12,14},{14,16},{16,18},{18... | collective-permute-start | bytes 786440 | tf_op jit(solution)/shard_map/ppermute | solution.py:24
  22.4 12.7 %collective-permute-start.1 = (bf16[256,512]{0,1:T(8,128)(2,1)}, bf16[256,512]{0,1:T(8,128)(2,1)}, u32[]{:S(2)}, u32[]{:S(2)}) collective-permute-start(bf16[256,512]{0,1:T(8,128)(2,1)} %get-tuple-element.76), channel_id=1, source_target_pairs={{2,0},{4,2},{6,4},{8,6},{10,8},{12,10},{14,12},{16,14},{18,16},{20... | collective-permute-start | bytes 786440 | tf_op jit(solution)/shard_map/ppermute | solution.py:26
  23.9 11.2 %copy-start.9 = (bf16[2048,256]{0,1:T(8,128)(2,1)S(1)}, bf16[2048,256]{0,1:T(8,128)(2,1)}, u32[]{:S(2)}) copy-start(bf16[2048,256]{0,1:T(8,128)(2,1)} %copy-done.8) | copy-start | bytes 3145732
  23.9 11.2 %copy-start.11 = (bf16[2048,256]{0,1:T(8,128)(2,1)S(1)}, bf16[2048,256]{0,1:T(8,128)(2,1)}, u32[]{:S(2)}) copy-start(bf16[2048,256]{0,1:T(8,128)(2,1)} %copy-done.10) | copy-start | bytes 3145732
  30.7 20.8 %copy-start.38 = (bf16[512,256]{0,1:T(8,128)(2,1)}, bf16[512,256]{0,1:T(8,128)(2,1)S(1)}, u32[]{:S(2)}) copy-start(bf16[512,256]{0,1:T(8,128)(2,1)S(1)} %get-tuple-element.88) | copy-start | bytes 786436
  93.7 25.1 %copy-start.55 = (f32[512]{0:T(512)S(1)}, f32[512]{0:T(512)}, u32[]{:S(2)}) copy-start(f32[512]{0:T(512)} %param.27) | copy-start | bytes 6148
  93.7 61.6 %all-reduce.11.cloned.1.call-start = ((), (), s32[]{:S(2)}) async-start(), calls=%async_computation.2 | async-start | bytes 4194304 | tf_op jit(solution)/shard_map/psum | solution.py:180
  132.7 401.9 %all-reduce.13.cloned.1.call-start = ((), (), s32[]{:S(2)}) async-start(), calls=%async_computation.4 | async-start | bytes 6291456 | tf_op jit(solution)/shard_map/psum | solution.py:244
  172.3 22.1 %copy-start.44 = (bf16[512,256]{0,1:T(8,128)(2,1)S(1)}, bf16[512,256]{0,1:T(8,128)(2,1)}, u32[]{:S(2)}) copy-start(bf16[512,256]{0,1:T(8,128)(2,1)} %get-tuple-element.90) | copy-start | bytes 786436
  222.6 21.9 %copy-start.42 = (bf16[512,256]{0,1:T(8,128)(2,1)S(1)}, bf16[512,256]{0,1:T(8,128)(2,1)}, u32[]{:S(2)}) copy-start(bf16[512,256]{0,1:T(8,128)(2,1)} %get-tuple-element.89) | copy-start | bytes 786436
  244.5 18.5 %copy-start.71 = (f32[4,512]{1,0:T(4,128)S(1)}, f32[4,512]{1,0:T(4,128)}, u32[]{:S(2)}) copy-start(f32[4,512]{1,0:T(4,128)} %copy-done.70) | copy-start | bytes 24580
  272.0 21.9 %copy-start.40 = (bf16[512,256]{0,1:T(8,128)(2,1)S(1)}, bf16[512,256]{0,1:T(8,128)(2,1)}, u32[]{:S(2)}) copy-start(bf16[512,256]{0,1:T(8,128)(2,1)} %get-tuple-element.87) | copy-start | bytes 786436
  293.9 18.3 %copy-start.69 = (f32[4,512]{1,0:T(4,128)S(1)}, f32[4,512]{1,0:T(4,128)}, u32[]{:S(2)}) copy-start(f32[4,512]{1,0:T(4,128)} %copy-done.68) | copy-start | bytes 24580
  321.1 21.9 %copy-start.39 = (bf16[512,256]{0,1:T(8,128)(2,1)S(1)}, bf16[512,256]{0,1:T(8,128)(2,1)}, u32[]{:S(2)}) copy-start(bf16[512,256]{0,1:T(8,128)(2,1)} %copy-done.38) | copy-start | bytes 786436
  343.0 18.6 %copy-start.22 = (f32[4,64,1024]{2,1,0:T(8,128)S(1)}, f32[4,64,1024]{2,1,0:T(8,128)}, u32[]{:S(2)}) copy-start(f32[4,64,1024]{2,1,0:T(8,128)} %fusion.44) | copy-start | bytes 3145732
  365.0 6.9 %copy-start.4 = (bf16[2048,512]{1,0:T(8,128)(2,1)S(1)}, bf16[2048,512]{1,0:T(8,128)(2,1)}, u32[]{:S(2)}) copy-start(bf16[2048,512]{1,0:T(8,128)(2,1)} %copy-done.3) | copy-start | bytes 6291460
  365.0 6.9 %copy-start.46 = (bf16[4,64,512]{2,1,0:T(8,128)(2,1)S(1)}, bf16[4,64,512]{2,1,0:T(8,128)(2,1)}, u32[]{:S(2)}) copy-start(bf16[4,64,512]{2,1,0:T(8,128)(2,1)} %fusion.110) | copy-start | bytes 786436
  365.0 6.9 %copy-start.47 = (bf16[4,64,512]{2,1,0:T(8,128)(2,1)S(1)}, bf16[4,64,512]{2,1,0:T(8,128)(2,1)}, u32[]{:S(2)}) copy-start(bf16[4,64,512]{2,1,0:T(8,128)(2,1)} %fusion.107) | copy-start | bytes 786436
  365.0 6.9 %copy-start.49 = (bf16[4,64,512]{2,1,0:T(8,128)(2,1)S(1)}, bf16[4,64,512]{2,1,0:T(8,128)(2,1)}, u32[]{:S(2)}) copy-start(bf16[4,64,512]{2,1,0:T(8,128)(2,1)} %fusion.113) | copy-start | bytes 786436
  365.0 6.9 %copy-start.51 = (bf16[4,64,512]{2,1,0:T(8,128)(2,1)S(1)}, bf16[4,64,512]{2,1,0:T(8,128)(2,1)}, u32[]{:S(2)}) copy-start(bf16[4,64,512]{2,1,0:T(8,128)(2,1)} %fusion.104) | copy-start | bytes 786436
  366.0 11.1 %collective-permute-start.3 = (bf16[256,512]{0,1:T(8,128)(2,1)S(1)}, bf16[256,512]{0,1:T(8,128)(2,1)S(1)}, u32[]{:S(2)}, u32[]{:S(2)}) collective-permute-start(bf16[256,512]{0,1:T(8,128)(2,1)S(1)} %slice.275), channel_id=1, source_target_pairs={{2,0},{4,2},{6,4},{8,6},{10,8},{12,10},{14,12},{16,14},{18,16},{20... | collective-permute-start | bytes 786440 | tf_op jit(solution)/shard_map/ppermute | solution.py:26
  367.3 15.8 %collective-permute-start.2 = (bf16[256,512]{0,1:T(8,128)(2,1)S(1)}, bf16[256,512]{0,1:T(8,128)(2,1)S(1)}, u32[]{:S(2)}, u32[]{:S(2)}) collective-permute-start(bf16[256,512]{0,1:T(8,128)(2,1)S(1)} %slice.276), channel_id=1, source_target_pairs={{0,2},{2,4},{4,6},{6,8},{8,10},{10,12},{12,14},{14,16},{16,18},{18... | collective-permute-start | bytes 786440 | tf_op jit(solution)/shard_map/ppermute | solution.py:24
  386.6 159.8 %reduce-scatter.2.cloned.1.call-start = ((), (), s32[]{:S(2)}) async-start(), calls=%async_computation.3 | async-start | bytes 3145728 | tf_op jit(solution)/shard_map/reduce_scatter | solution.py:234
  534.5 10.2 %copy-start.20 = (bf16[1024,512]{1,0:T(8,128)(2,1)S(1)}, bf16[1024,512]{1,0:T(8,128)(2,1)}, u32[]{:S(2)}) copy-start(bf16[1024,512]{1,0:T(8,128)(2,1)} %get-tuple-element.64) | copy-start | bytes 3145732
  536.4 9.9 %copy-start.54 = (f32[512]{0:T(512)S(1)}, f32[512]{0:T(512)}, u32[]{:S(2)}) copy-start(f32[512]{0:T(512)} %param.22) | copy-start | bytes 6148
  541.8 7.0 %dynamic-slice-start = ((f32[2048]{0:T(1024)}, s32[]{:T(128)}), f32[1024]{0:T(1024)S(1)}, s32[]{:S(2)}) async-start(f32[2048]{0:T(1024)} %copy-done.52, s32[]{:T(128)} %select_n.30), calls=%async_computation.5 | async-start | bytes 8704 | tf_op jit(solution)/shard_map/dynamic-slice.31
  546.3 6.9 %copy-start.1 = (bf16[512,1024]{1,0:T(8,128)(2,1)S(1)}, bf16[512,1024]{1,0:T(8,128)(2,1)}, u32[]{:S(2)}) copy-start(bf16[512,1024]{1,0:T(8,128)(2,1)} %param.28) | copy-start | bytes 3145732
  (51 other events, 178.9 us)
Sparse Core Ops, SparseCore 0:
  93.8 21.5 all-reduce.8
  132.8 22.4 all-reduce.10
  386.7 147.7 all-reduce.12
  537.2 8.6 reduce-scatter.1
where the time goes:
time: 564 us; the launch traced here: 560 us
  matrix products  287 us (51%)
  waiting for transfers between devices  191 us (34%)
  other arithmetic  46 us (8%)
  between operations  14.8 us (3%)
  starting transfers between devices  13.3 us (2%)
  local copies, waits for them, and re-layouts  7.43 us (1%)
    psum x1, waiting for transfers between devices, local(): lax.psum(grad_query_terms.astype(jnp.bfloat16), 'tm').astype(jnp.float32)  143 us
    dot_general x8, matrix products, key_grads(): jnp.einsum('hqk,qhd->khd', score_tile, query_block, preferred_element_typ...  89.7 us
    dot_general x4, matrix products, query_grads(): jnp.einsum('hqk,khd->qhd', score_tile, key_tile, preferred_element_type=j...  87.9 us
    sub x4, matrix products, softmax_rows(): weights = jnp.exp(scores - peak)  30.2 us
    dot_general x4, matrix products, block_context(): jnp.einsum('hqk,khd->qhd', probability.astype(jnp.bfloat16), value_block,...  22.4 us
    psum x1, waiting for transfers between devices, local(): lax.psum(partial_value.astype(jnp.bfloat16), 'ffn').astype(jnp.float32)  21.5 us
    dot_general x4, matrix products, score_grads(): jnp.einsum('qhd,khd->hqk', grad_block, value_tile, preferred_element_type...  18.1 us
    psum x1, waiting for transfers between devices, local(): lax.psum(grad_second_part.astype(jnp.bfloat16), 'ffn').astype(jnp.float32)  12.7 us
  transfers between devices with their start and end apart: 8, of which 7 were waited for; matrix products, arithmetic and copies ran while one was open for 6% of the time, Pallas kernels for 0%

commit v1 on v0

v1 whole, which is shorter than its diff:
```python
import math

import jax
import jax.numpy as jnp
from jax import lax
from jax.experimental import pallas as pl
from jax.experimental.pallas import tpu as pltpu
from jax.sharding import PartitionSpec as P

HEAD_DIM = 64
HALF = 256


epsilon = 1e-05
masked_score = -1e30


def with_halo(cells, sides, width):
    for axis, dim in sides:
        count = lax.axis_size(axis)
        ends = count - 1
        head = lax.slice_in_dim(cells, 0, width, axis=dim)
        tail = lax.slice_in_dim(cells, cells.shape[dim] - width, cells.shape[dim], axis=dim)
        cells = jnp.concatenate(
            [
                lax.ppermute(tail, axis, [(i, (i + 1) % count) for i in range(ends)]),
                cells,
                lax.ppermute(head, axis, [((i + 1) % count, i) for i in range(ends)]),
            ],
            axis=dim,
        )
    return cells


def layer_norm(inputs):
    center = jnp.mean(inputs, axis=-1, keepdims=True)
    shifted = inputs - center
    inverse = lax.rsqrt(jnp.mean(shifted * shifted, axis=-1, keepdims=True) + epsilon)
    return (shifted * inverse, inverse)


def norm_back(grad_normed, scaled, inverse, gain):
    weighted = grad_normed * gain
    first_mean = jnp.mean(weighted, axis=-1, keepdims=True)
    second_mean = jnp.mean(weighted * scaled, axis=-1, keepdims=True)
    return inverse * (weighted - first_mean - scaled * second_mean)


def project(normed, weight):
    return jnp.dot(normed, weight, preferred_element_type=jnp.float32).astype(jnp.bfloat16)


def contract(left, right, dims):
    return lax.dot_general(left, right, (dims, ((), ())), preferred_element_type=jnp.float32)


def window_bias(record_query_ref, record_key_ref, start, rows, window):
    key_ids = record_key_ref[pl.ds(start, window), :]
    query_ids = record_query_ref[...]
    offsets = lax.broadcasted_iota(jnp.int32, (window, rows), 0) - lax.broadcasted_iota(
        jnp.int32, (window, rows), 1
    )
    allowed = (offsets >= 0) & (offsets < 2 * HALF) & (key_ids == query_ids)
    return jnp.where(allowed, 0.0, masked_score)


def head_mask(head, value):
    lanes = lax.broadcasted_iota(jnp.int32, (1, 2 * HEAD_DIM), 1)
    own = (lanes >= head * HEAD_DIM) & (lanes < (head + 1) * HEAD_DIM)
    return jnp.where(own, value, 0.0).astype(jnp.bfloat16)


def forward_kernel(query_ref, pair_ref, record_query_ref, record_key_ref, context_ref, lse_ref):
    rows, cols = query_ref.shape
    window = rows + 2 * HALF
    start = pl.multiple_of(pl.program_id(0) * rows, rows)
    bias = window_bias(record_query_ref, record_key_ref, start, rows, window)
    width = 2 * HEAD_DIM
    for pair in range(cols // width):
        lanes = slice(pair * width, (pair + 1) * width)
        key_tile = pair_ref[pl.ds(start, window), lanes]
        value_t = pair_ref[pl.ds(start, window), cols + pair * width : cols + (pair + 1) * width].T
        query_tile = query_ref[:, lanes]
        parts = []
        for head in range(2):
            query_head = query_tile * head_mask(head, HEAD_DIM ** (-0.5))
            scores = contract(key_tile, query_head, ((1,), (1,))) + bias
            peak = jnp.max(scores, axis=0, keepdims=True)
            weights = jnp.exp(scores - peak)
            total = jnp.sum(weights, axis=0, keepdims=True)
            mixed = contract(
                value_t[head * HEAD_DIM : (head + 1) * HEAD_DIM],
                weights.astype(jnp.bfloat16),
                ((1,), (0,)),
            )
            parts.append(mixed * (1.0 / total))
            lse_ref[2 * pair + head : 2 * pair + head + 1, :] = peak + jnp.log(total)
        context_ref[:, lanes] = jnp.concatenate(parts, axis=0).T.astype(jnp.bfloat16)


def backward_kernel(
    query_ref,
    pair_ref,
    grad_ref,
    lse_ref,
    record_query_ref,
    record_key_ref,
    grad_query_ref,
    own_ref,
    own_rim_ref,
    sent_rim_ref,
    total_ref,
):
    rows, cols = query_ref.shape
    window = rows + 2 * HALF
    step = pl.program_id(0)
    start = pl.multiple_of(step * rows, rows)
    width = 2 * HEAD_DIM

    @pl.when(step == 0)
    def _():
        total_ref[...] = jnp.zeros_like(total_ref)

    bias = window_bias(record_query_ref, record_key_ref, start, rows, window)
    for pair in range(cols // width):
        lanes = slice(pair * width, (pair + 1) * width)
        value_lanes = slice(cols + pair * width, cols + (pair + 1) * width)
        key_tile = pair_ref[pl.ds(start, window), lanes]
        value_tile = pair_ref[pl.ds(start, window), value_lanes]
        key_t = key_tile.T
        parts = []
        grad_key = None
        for head in range(2):
            query_head = query_ref[:, lanes] * head_mask(head, HEAD_DIM ** (-0.5))
            grad_head = grad_ref[:, lanes] * head_mask(head, 1.0)
            scores = contract(key_tile, query_head, ((1,), (1,))) + bias
            index = 2 * pair + head
            probability = jnp.exp(scores - lse_ref[index : index + 1, :])
            grad_prob = contract(value_tile, grad_head, ((1,), (1,)))
            inner = jnp.sum(probability * grad_prob, axis=0, keepdims=True)
            grad_scores = (probability * (grad_prob - inner)).astype(jnp.bfloat16)
            value_term = contract(probability.astype(jnp.bfloat16), grad_head, ((1,), (0,)))
            key_term = contract(grad_scores, query_head, ((1,), (0,)))
            grad_key = key_term if grad_key is None else grad_key + key_term
            grad_value = value_term if head == 0 else grad_value + value_term
            parts.append(
                contract(
                    key_t[head * HEAD_DIM : (head + 1) * HEAD_DIM], grad_scores, ((1,), (0,))
                )
            )
        grad_query = jnp.concatenate(parts, axis=0).T * HEAD_DIM ** (-0.5)
        grad_query_ref[:, lanes] = grad_query.astype(jnp.bfloat16)
        total_ref[pl.ds(start, window), lanes] += grad_key
        total_ref[pl.ds(start, window), value_lanes] += grad_value

    @pl.when(step == pl.num_programs(0) - 1)
    def _():
        slab = own_ref.shape[0]
        own_ref[...] = total_ref[HALF : HALF + slab, :].astype(jnp.bfloat16)
        own_rim_ref[:HALF] = total_ref[HALF : 2 * HALF, :]
        own_rim_ref[HALF:] = total_ref[slab : slab + HALF, :]
        sent_rim_ref[:HALF] = total_ref[:HALF, :].astype(jnp.bfloat16)
        sent_rim_ref[HALF:] = total_ref[slab + HALF :, :].astype(jnp.bfloat16)


def whole(shape):
    return pl.BlockSpec(shape, lambda i: (0, 0))


def attention_forward(queries, pairs, record_query, record_key):
    slab, cols = queries.shape
    heads = cols // HEAD_DIM
    rows = HALF
    return pl.pallas_call(
        forward_kernel,
        grid=(slab // rows,),
        in_specs=[
            pl.BlockSpec((rows, cols), lambda i: (i, 0)),
            whole(pairs.shape),
            pl.BlockSpec((1, rows), lambda i: (0, i)),
            whole(record_key.shape),
        ],
        out_specs=[
            pl.BlockSpec((rows, cols), lambda i: (i, 0)),
            pl.BlockSpec((heads, rows), lambda i: (0, i)),
        ],
        out_shape=[
            jax.ShapeDtypeStruct((slab, cols), jnp.bfloat16),
            jax.ShapeDtypeStruct((heads, slab), jnp.float32),
        ],
        cost_estimate=pl.CostEstimate(
            flops=4 * slab * 3 * HALF * cols * 4,
            bytes_accessed=slab * cols * 8,
            transcendentals=slab * 3 * HALF * heads,
        ),
        name="attention_forward",
    )(queries, pairs, record_query, record_key)


def attention_backward(queries, pairs, grad_context, lse, record_query, record_key):
    slab, cols = queries.shape
    heads = cols // HEAD_DIM
    rows = HALF
    return pl.pallas_call(
        backward_kernel,
        grid=(slab // rows,),
        in_specs=[
            pl.BlockSpec((rows, cols), lambda i: (i, 0)),
            whole(pairs.shape),
            pl.BlockSpec((rows, cols), lambda i: (i, 0)),
            pl.BlockSpec((heads, rows), lambda i: (0, i)),
            pl.BlockSpec((1, rows), lambda i: (0, i)),
            whole(record_key.shape),
        ],
        out_specs=[
            pl.BlockSpec((rows, cols), lambda i: (i, 0)),
            whole((slab, 2 * cols)),
            whole((2 * HALF, 2 * cols)),
            whole((2 * HALF, 2 * cols)),
        ],
        out_shape=[
            jax.ShapeDtypeStruct((slab, cols), jnp.bfloat16),
            jax.ShapeDtypeStruct((slab, 2 * cols), jnp.bfloat16),
            jax.ShapeDtypeStruct((2 * HALF, 2 * cols), jnp.float32),
            jax.ShapeDtypeStruct((2 * HALF, 2 * cols), jnp.bfloat16),
        ],
        scratch_shapes=[pltpu.VMEM(pairs.shape, jnp.float32)],
        cost_estimate=pl.CostEstimate(
            flops=10 * slab * 3 * HALF * cols * 4,
            bytes_accessed=slab * cols * 16,
            transcendentals=slab * 3 * HALF * heads,
        ),
        name="attention_backward",
    )(queries, pairs, grad_context, lse, record_query, record_key)


def shift(array, axis, by):
    count = lax.axis_size(axis)
    return lax.ppermute(array, axis, [(i, (i + by) % count) for i in range(count)])


def group_sum(term):
    low = term.astype(jnp.bfloat16)
    total = low.astype(jnp.float32)
    for by in range(1, lax.axis_size("ffn")):
        total = total + shift(low, "ffn", by).astype(jnp.float32)
    return total


def group_scatter(term):
    low = term.astype(jnp.bfloat16)
    count = lax.axis_size("ffn")
    rows = low.shape[0] // count
    me = lax.axis_index("ffn")
    total = lax.dynamic_slice_in_dim(low, me * rows, rows, 0).astype(jnp.float32)
    for by in range(1, count):
        piece = lax.dynamic_slice_in_dim(low, ((me + by) % count) * rows, rows, 0)
        total = total + shift(piece, "ffn", by).astype(jnp.float32)
    return total


def local(
    frames,
    upstream,
    recording,
    first_gain,
    query_weight,
    key_weight,
    value_weight,
    out_weight,
    second_gain,
    inner_weight,
    outer_weight,
):
    slab_rows = frames.shape[0]
    head_cols = query_weight.shape[1]
    share_rows = slab_rows // lax.axis_size("ffn")
    share_start = lax.axis_index("ffn") * share_rows
    record_pad = jnp.pad(recording, (HALF, HALF), constant_values=-1)
    record_ext = lax.dynamic_slice_in_dim(
        record_pad, lax.axis_index("tm") * slab_rows, slab_rows + 2 * HALF
    )
    frames_wide = frames.astype(jnp.float32)
    upstream_wide = upstream.astype(jnp.float32)
    scaled_first, inverse_first = layer_norm(frames_wide)
    normed_first = (scaled_first * first_gain).astype(jnp.bfloat16)
    queries = project(normed_first, query_weight)
    key_rows = project(normed_first, key_weight)
    value_rows = project(normed_first, value_weight)
    key_value = jnp.concatenate([key_rows, value_rows], axis=1)
    key_value_ext = with_halo(key_value, (("tm", 0),), HALF)
    record_query = record_ext[HALF : HALF + slab_rows].reshape(1, slab_rows)
    record_key = record_ext.reshape(slab_rows + 2 * HALF, 1)
    context, lse = attention_forward(queries, key_value_ext, record_query, record_key)
    partial_value = jnp.dot(context, out_weight, preferred_element_type=jnp.float32)
    middle = frames_wide + group_sum(partial_value)
    scaled_second, inverse_second = layer_norm(middle)
    normed_second = (scaled_second * second_gain).astype(jnp.bfloat16)
    inner_pre = jnp.dot(normed_second, inner_weight, preferred_element_type=jnp.float32)
    activation = jax.nn.silu(inner_pre).astype(jnp.bfloat16)
    sigmoid_inner = jax.nn.sigmoid(inner_pre)
    grad_act = jnp.dot(upstream, outer_weight.T, preferred_element_type=jnp.float32) * 0.5
    grad_inner = (grad_act * sigmoid_inner * (1.0 + inner_pre * (1.0 - sigmoid_inner))).astype(
        jnp.bfloat16
    )
    grad_outer_terms = jnp.dot(activation.T, upstream, preferred_element_type=jnp.float32) * 0.5
    grad_inner_terms = jnp.dot(normed_second.T, grad_inner, preferred_element_type=jnp.float32)
    grad_second_part = jnp.dot(grad_inner, inner_weight.T, preferred_element_type=jnp.float32)
    grad_second = group_sum(grad_second_part)
    grad_middle = upstream_wide + norm_back(grad_second, scaled_second, inverse_second, second_gain)
    grad_middle_low = grad_middle.astype(jnp.bfloat16)
    grad_middle_share = lax.dynamic_slice_in_dim(grad_middle, share_start, share_rows, 0)
    grad_out_terms = jnp.dot(context.T, grad_middle_low, preferred_element_type=jnp.float32)
    grad_context = jnp.dot(
        grad_middle_low, out_weight.T, preferred_element_type=jnp.float32
    ).astype(jnp.bfloat16)
    grad_query_low, own, own_rim, sent_rim = attention_backward(
        queries, key_value_ext, grad_context, lse, record_query, record_key
    )
    count = lax.axis_size("tm")
    from_lower = lax.ppermute(sent_rim[HALF:], "tm", [(i, i + 1) for i in range(count - 1)])
    from_upper = lax.ppermute(sent_rim[:HALF], "tm", [(i + 1, i) for i in range(count - 1)])
    grad_pairs = jnp.concatenate(
        [
            (own_rim[:HALF] + from_lower.astype(jnp.float32)).astype(jnp.bfloat16),
            own[HALF : slab_rows - HALF],
            (own_rim[HALF:] + from_upper.astype(jnp.float32)).astype(jnp.bfloat16),
        ],
        axis=0,
    )
    grad_key_low = grad_pairs[:, :head_cols]
    grad_value_low = grad_pairs[:, head_cols:]
    grad_query_terms = jnp.dot(normed_first.T, grad_query_low, preferred_element_type=jnp.float32)
    grad_key_terms = jnp.dot(normed_first.T, grad_key_low, preferred_element_type=jnp.float32)
    grad_value_terms = jnp.dot(normed_first.T, grad_value_low, preferred_element_type=jnp.float32)
    grad_first_part = jnp.dot(grad_query_low, query_weight.T, preferred_element_type=jnp.float32)
    grad_first_part = grad_first_part + jnp.dot(
        grad_key_low, key_weight.T, preferred_element_type=jnp.float32
    )
    grad_first_part = grad_first_part + jnp.dot(
        grad_value_low, value_weight.T, preferred_element_type=jnp.float32
    )
    grad_first_share = group_scatter(grad_first_part)
    scaled_share = lax.dynamic_slice_in_dim(scaled_first, share_start, share_rows, 0)
    inverse_share = lax.dynamic_slice_in_dim(inverse_first, share_start, share_rows, 0)
    grad_frames = grad_middle_share + norm_back(
        grad_first_share, scaled_share, inverse_share, first_gain
    )
    weight_scale = 1.0 / math.sqrt(recording.shape[0])
    first_totals = lax.psum(
        (grad_inner_terms.astype(jnp.bfloat16), grad_outer_terms.astype(jnp.bfloat16)), "tm"
    )
    attention_terms = tuple(
        term.astype(jnp.bfloat16)
        for term in (grad_query_terms, grad_key_terms, grad_value_terms, grad_out_terms)
    )
    attention_terms, first_totals = lax.optimization_barrier((attention_terms, first_totals))
    totals = tuple(
        total.astype(jnp.float32) for total in lax.psum(attention_terms, "tm") + first_totals
    )
    return (grad_frames,) + tuple((total * weight_scale for total in totals))


def solution(mesh):
    in_specs = (
        P("tm", None),
        P("tm", None),
        P(),
        P(),
        P(None, "ffn"),
        P(None, "ffn"),
        P(None, "ffn"),
        P("ffn", None),
        P(),
        P(None, "ffn"),
        P("ffn", None),
    )
    out_specs = (
        P(("tm", "ffn"), None),
        P(None, "ffn"),
        P(None, "ffn"),
        P(None, "ffn"),
        P("ffn", None),
        P(None, "ffn"),
        P("ffn", None),
    )
    return jax.shard_map(local, mesh=mesh, in_specs=in_specs, out_specs=out_specs, check_vma=False)
```

time: 564 us -> 368 us (0.65)
  matrix products: 287 us -> 45 us
  Pallas kernels: 0 us -> 51.4 us
  local copies, waits for them, and re-layouts: 7.43 us -> 18.9 us
  other arithmetic: 46 us -> 37.5 us
  waiting for transfers between devices: 191 us -> 184 us
    dot_general x20 -> x0, matrix products: 218 us -> none  [the longest x8 89.7 us: key_grads(): jnp.einsum('hqk,qhd->khd', score_tile, query_block, preferred_element_typ...]
    pallas_call x0 -> x2, Pallas kernels: none -> 51.4 us  [the longest x1 29.2 us: attention_backward(): pl.pallas_call(backward_kernel, grid=(slab // rows,), in_specs=[pl.BlockS...]
    sub x4 -> x0, matrix products: 30.2 us -> none  [softmax_rows(): weights = jnp.exp(scores - peak)]
    ppermute x0 -> x5, waiting for transfers between devices: none -> 7.88 us  [the longest x1 6.54 us: local(): lax.ppermute(sent_rim[HALF:], 'tm', [(i, i + 1) for i in range(count - 1)])]
    unnamed x148 -> x71, local copies, waits for them, and re-layouts: 6.15 us -> 13.7 us
    psum x3 -> x2, waiting for transfers between devices: 177 us -> 171 us  [the longest x1 110 us: local(): lax.psum(attention_terms, 'tm') + first_totals]
  transfers between devices with their start and end apart: 8 -> 9, of which waited for: 7 -> 7; matrix products, arithmetic and copies ran while one was open for 6% -> 16% of each run, Pallas kernels for 0% -> 8%
where the time goes in v1:
time: 368 us; the launch traced here: 364 us
  waiting for transfers between devices  184 us (50%)
  Pallas kernels  51.4 us (14%)
  matrix products  45 us (12%)
  other arithmetic  37.5 us (10%)
  local copies, waits for them, and re-layouts  18.9 us (5%)
  between operations  14.9 us (4%)
  starting transfers between devices  12.3 us (3%)
    psum x1, waiting for transfers between devices, local(): lax.psum(attention_terms, 'tm') + first_totals  110 us
    psum x1, waiting for transfers between devices, local(): lax.psum((grad_inner_terms.astype(jnp.bfloat16), grad_outer_terms.astype(...  60.6 us
    pallas_call x1, Pallas kernels, attention_backward(): pl.pallas_call(backward_kernel, grid=(slab // rows,), in_specs=[pl.BlockS...  29.2 us
    pallas_call x1, Pallas kernels, attention_forward(): pl.pallas_call(forward_kernel, grid=(slab // rows,), in_specs=[pl.BlockSp...  22.1 us
    unnamed x71, local copies, waits for them, and re-layouts  13.7 us
    mul x6, other arithmetic, local(): return (grad_frames,) + tuple((total * weight_scale for total in totals))  10.5 us
  transfers between devices with their start and end apart: 9, of which 7 were waited for; matrix products, arithmetic and copies ran while one was open for 16% of the time, Pallas kernels for 8%

profile of v1, /device:TPU:0, one launch (start us, length us, event | category | flops | bytes accessed | tf_op | source)
XLA Modules:
  0.0 364.3 jit_solution(790829231740284390)
XLA Ops:
  7.3 3.0 copy.24
  14.5 5.6 %collective-permute-start = (bf16[256,512]{1,0:T(8,128)(2,1)}, bf16[256,512]{1,0:T(8,128)(2,1)}, u32[]{:S(2)}, u32[]{:S(2)}) collective-permute-start(bf16[256,512]{1,0:T(8,128)(2,1)} %get-tuple-element.58), channel_id=1, source_target_pairs={{0,2},{2,4},{4,6},{6,8},{8,10},{10,12},{12,14},{14,16},{16,18},{18... | collective-permute-start | bytes 786440 | tf_op jit(solution)/shard_map/ppermute | solution.py:26
  21.6 2.0 reshape.79.record_key_ref
  24.3 2.7 convolution_convert_fusion.5.query_ref
  26.9 4.0 %collective-permute-done = bf16[256,512]{1,0:T(8,128)(2,1)} collective-permute-done((bf16[256,512]{1,0:T(8,128)(2,1)}, bf16[256,512]{1,0:T(8,128)(2,1)}, u32[]{:S(2)}, u32[]{:S(2)}) %collective-permute-start) | collective-permute-done | bytes 262176 | tf_op jit(solution)/shard_map/ppermute | solution.py:26
  30.9 1.9 collective-permute-done.1
  32.8 3.0 pad_maximum_fusion.pair_ref
  35.8 22.1 %attention_forward.1 = (bf16[2048,256]{1,0:T(8,128)(2,1)}, f32[4,2048]{1,0:T(4,128)}) custom-call(bf16[2048,256]{1,0:T(8,128)(2,1)} %convolution_convert_fusion.5.query_ref, bf16[2560,512]{1,0:T(8,128)(2,1)} %pad_maximum_fusion.pair_ref, s32[1,2048]{1,0:T(1,128)} %bitcast.20, s32[2560,1]{1,0:T(8,128)} %reshape.79.record_key_ref), custom_call_target="tpu_custom_call" | custom-call | flops 6442450944 | bytes 4194304 | tf_op jit(solution)/shard_map/attention_forward/pallas_call | solution.py:174
  58.0 3.3 convolution_convert_fusion.1
  61.3 3.9 %copy.23 = bf16[2048,512]{0,1:T(8,128)(2,1)} copy(bf16[2048,512]{1,0:T(8,128)(2,1)} %param.12) | data formatting | bytes 4194304 | tf_op args[1]
  65.8 5.7 %fusion.16 = (f32[2048]{0:T(1024)S(1)}, f32[2048,512]{0,1:T(8,128)S(1)}, f32[2048,512]{0,1:T(8,128)}) fusion(bf16[2048,512]{0,1:T(8,128)(2,1)} %collective-permute-done.2, bf16[2048,512]{0,1:T(8,128)(2,1)} %convolution_convert_fusion.1, bf16[2048,512]{0,1:T(8,128)(2,1)S(1)} %copy.24, f32[2048]{0:T(1024)S(1)} %add_rsqrt_fusion.1, ...), kind=kLoop, calls=%fused_computation.68 | loop fusion | flops 8386560 | bytes 14704640 | tf_op jit(solution)/shard_map/reduce_sum | solution.py:36
  72.2 2.5 fusion.15
  74.8 5.3 %multiply_convert_fusion.1 = bf16[2048,1024]{1,0:T(8,128)(2,1)S(1)} fusion(f32[2048,1024]{1,0:T(8,128)S(1)} %fusion.15, bf16[2048,512]{1,0:T(8,128)(2,1)S(1)} %copy-done.14, bf16[1024,512]{1,0:T(8,128)(2,1)S(1)} %copy-done.33), kind=kOutput, calls=%fused_computation.1 | convolution fusion | flops 2168455168 | bytes 15728640 | tf_op jit(solution)/shard_map/dot_general | solution.py:302
  80.1 3.7 %convolution_convert_fusion = bf16[2048,512]{0,1:T(8,128)(2,1)} fusion(bf16[2048,1024]{1,0:T(8,128)(2,1)S(1)} %multiply_convert_fusion.1, bf16[512,1024]{1,0:T(8,128)(2,1)S(1)} %copy-done), kind=kOutput, calls=%fused_computation.19 | convolution fusion | flops 2148532224 | bytes 7340032 | tf_op jit(solution)/shard_map/dot_general | solution.py:308
  83.9 3.4 convolution_convert_fusion.6
  87.3 3.5 multiply_convert_fusion.5
  90.9 5.0 %fusion.4 = (f32[2048]{0:T(1024)S(1)}, f32[2048]{0:T(1024)S(1)}) fusion(bf16[2048,512]{0,1:T(8,128)(2,1)} %collective-permute-done.3, bf16[2048,512]{0,1:T(8,128)(2,1)} %convolution_convert_fusion, f32[512]{0:T(512)S(1)} %copy-done.32, f32[2048]{0:T(1024)S(1)} %add_rsqrt_fusion, f32[2048,512]{0,1:T(8,128)} %copy-done.2, f32[2048]{0:T(1024)S(1)} %broadcast_multiply_fusion.2), kind=kLoop, calls=%fused_computation.18 | loop fusion | flops 9433088 | bytes 8423424 | tf_op jit(solution)/shard_map/reduce_sum | solution.py:44
  96.2 4.4 %multiply_add_fusion = f32[2048,512]{0,1:T(8,128)S(1)} fusion(bf16[2048,512]{0,1:T(8,128)(2,1)S(1)} %copy-done.7, f32[2048,512]{0,1:T(8,128)S(1)} %copy-done.3, bf16[2048,512]{0,1:T(8,128)(2,1)} %collective-permute-done.3, bf16[2048,512]{0,1:T(8,128)(2,1)} %convolution_convert_fusion, f32[2048]{0:T(1024)S(1)} %get-tuple-element.64, ...), kind=kLoop, calls=%fused_computation.10 | loop fusion | flops 12582912 | bytes 14714880 | tf_op jit(solution)/shard_map/add | solution.py:310
  100.6 2.0 copy-done.4
  104.3 29.2 %attention_backward.1 = (bf16[2048,256]{1,0:T(8,128)(2,1)}, bf16[2048,512]{1,0:T(8,128)(2,1)}, f32[512,512]{1,0:T(8,128)}, bf16[512,512]{1,0:T(8,128)(2,1)}) custom-call(bf16[2048,256]{1,0:T(8,128)(2,1)} %convolution_convert_fusion.5.query_ref, bf16[2560,512]{1,0:T(8,128)(2,1)} %pad_maximum_fusion.pair_ref, ...), custom_call_target="tpu_custom_call" | custom-call | flops 16106127360 | bytes 8388608 | tf_op jit(solution)/shard_map/attention_backward/pallas_call | solution.py:204
  134.8 3.8 %collective-permute-start.4 = (bf16[256,512]{1,0:T(8,128)(2,1)S(1)}, bf16[256,512]{1,0:T(8,128)(2,1)S(1)}, u32[]{:S(2)}, u32[]{:S(2)}) collective-permute-start(bf16[256,512]{1,0:T(8,128)(2,1)S(1)} %get-tuple-element.62), channel_id=1, source_target_pairs={{0,2},{2,4},{4,6},{6,8},{8,10},{10,12},{12,14},{14,16},{16,18},{18... | collective-permute-start | bytes 786440 | tf_op jit(solution)/shard_map/ppermute | solution.py:321
  139.9 2.8 convolution_convert_fusion.10
  144.4 6.5 %collective-permute-done.4 = bf16[256,512]{1,0:T(8,128)(2,1)S(1)} collective-permute-done((bf16[256,512]{1,0:T(8,128)(2,1)S(1)}, bf16[256,512]{1,0:T(8,128)(2,1)S(1)}, u32[]{:S(2)}, u32[]{:S(2)}) %collective-permute-start.4) | collective-permute-done | bytes 262176 | tf_op jit(solution)/shard_map/ppermute | solution.py:321
  152.0 2.7 fusion.12
  154.7 2.7 fusion.9
  160.5 60.6 %all-reduce.8.cloned.1.call-done = (bf16[512,1024]{1,0:T(8,128)(2,1)}, bf16[1024,512]{1,0:T(8,128)(2,1)}) async-done(((bf16[512,1024]{1,0:T(8,128)(2,1)}, bf16[1024,512]{1,0:T(8,128)(2,1)}), (bf16[512,1024]{1,0:T(8,128)(2,1)}, bf16[1024,512]{1,0:T(8,128)(2,1)})) %all-reduce.8.cloned.1.call-update) | async-done | bytes 2097168 | tf_op jit(solution)/shard_map/psum | solution.py:350
  221.1 4.3 %add_convert_fusion = bf16[2048,512]{0,1:T(8,128)(2,1)S(1)} fusion(f32[2048,512]{0,1:T(8,128)} %fusion.9, f32[2048,512]{0,1:T(8,128)} %fusion.12, bf16[2048,256]{1,0:T(8,128)(2,1)S(1)} %copy-done.18, bf16[512,256]{1,0:T(8,128)(2,1)S(1)} %copy-done.27), kind=kOutput, calls=%fused_computation.9 | convolution fusion | flops 540016640 | bytes 11796480 | tf_op jit(solution)/shard_map/dot_general | solution.py:336
  229.7 110.0 %all-reduce.6.cloned.1.call-done = (bf16[512,256]{1,0:T(8,128)(2,1)}, bf16[512,256]{1,0:T(8,128)(2,1)}, bf16[512,256]{1,0:T(8,128)(2,1)}, bf16[256,512]{1,0:T(8,128)(2,1)}) async-done(((bf16[512,256]{1,0:T(8,128)(2,1)}, bf16[512,256]{1,0:T(8,128)(2,1)}, bf16[512,256]{1,0:T(8,128)(2,1)}, bf16[256,512]{1,0:T(8,128)(2,1)}), (bf16[512,256]{1,0:T(8,128)(2,1)}, bf16[512,256]{1,0:T(8,128)(2,1)}, ...) | async-done | bytes 1048592 | tf_op jit(solution)/shard_map/psum | solution.py:359
  339.8 2.0 convert_multiply_fusion.2
  348.1 2.1 fusion.5
  350.2 4.0 %multiply_add_fusion.1 = f32[1024,512]{0,1:T(8,128)} fusion(f32[2048,512]{0,1:T(8,128)S(1)} %copy-done.6, s32[]{:T(128)} %select_n.20, f32[2048,512]{0,1:T(8,128)} %get-tuple-element.57, bf16[1024,512]{0,1:T(8,128)(2,1)} %copy-done.12, f32[1024]{0:T(1024)S(1)} %broadcast_multiply_fusion.4, f32[1024]{0:T(1024)S(1)} %broadcast_multiply_fusion.5, ...), kind=kLoop, calls=%fused_computation.30 | loop fusion | flops 4718592 | bytes 8402948 | tf_op jit(solution)/shard_map/add | solution.py:346
  354.2 2.9 copy.29
  (111 shorter events, 29.0 us)
Async XLA Ops:
  7.2 64.9 %copy-start = (bf16[512,1024]{1,0:T(8,128)(2,1)S(1)}, bf16[512,1024]{1,0:T(8,128)(2,1)}, u32[]{:S(2)}) copy-start(bf16[512,1024]{1,0:T(8,128)(2,1)} %param.20) | copy-start | bytes 3145732
  7.2 4.1 %copy-start.29 = (f32[512]{0:T(512)S(1)}, f32[512]{0:T(512)}, u32[]{:S(2)}) copy-start(f32[512]{0:T(512)} %param.14) | copy-start | bytes 6148
  7.2 4.1 %copy-start.22 = (bf16[512,256]{1,0:T(8,128)(2,1)S(1)}, bf16[512,256]{1,0:T(8,128)(2,1)}, u32[]{:S(2)}) copy-start(bf16[512,256]{1,0:T(8,128)(2,1)} %param.16) | copy-start | bytes 786436
  7.2 213.8 %all-reduce.8.cloned.1.call-start = ((), (), s32[]{:S(2)}) async-start(), calls=%async_computation.1 | async-start | bytes 4194304 | tf_op jit(solution)/shard_map/psum | solution.py:350
  11.3 147.7 %copy-start.28 = (f32[2048]{0:T(1024)}, f32[2048]{0:T(1024)S(1)}, u32[]{:S(2)}) copy-start(f32[2048]{0:T(1024)S(1)} %add_rsqrt_fusion.1) | copy-start | bytes 24580
  12.3 9.2 %copy-start.21 = (s32[32768]{0:T(1024)S(1)}, s32[32768]{0:T(1024)}, u32[]{:S(2)}) copy-start(s32[32768]{0:T(1024)} %param.13) | copy-start | bytes 393220
  12.3 11.9 %copy-start.26 = (bf16[512,256]{1,0:T(8,128)(2,1)S(1)}, bf16[512,256]{1,0:T(8,128)(2,1)}, u32[]{:S(2)}) copy-start(bf16[512,256]{1,0:T(8,128)(2,1)} %param.15) | copy-start | bytes 786436
  14.5 16.4 %collective-permute-start = (bf16[256,512]{1,0:T(8,128)(2,1)}, bf16[256,512]{1,0:T(8,128)(2,1)}, u32[]{:S(2)}, u32[]{:S(2)}) collective-permute-start(bf16[256,512]{1,0:T(8,128)(2,1)} %get-tuple-element.58), channel_id=1, source_target_pairs={{0,2},{2,4},{4,6},{6,8},{8,10},{10,12},{12,14},{14,16},{16,18},{18... | collective-permute-start | bytes 786440 | tf_op jit(solution)/shard_map/ppermute | solution.py:26
  20.1 12.7 %collective-permute-start.1 = (bf16[256,512]{1,0:T(8,128)(2,1)}, bf16[256,512]{1,0:T(8,128)(2,1)}, u32[]{:S(2)}, u32[]{:S(2)}) collective-permute-start(bf16[256,512]{1,0:T(8,128)(2,1)} %get-tuple-element.59), channel_id=1, source_target_pairs={{2,0},{4,2},{6,4},{8,6},{10,8},{12,10},{14,12},{16,14},{18,16},{20... | collective-permute-start | bytes 786440 | tf_op jit(solution)/shard_map/ppermute | solution.py:28
  23.6 9.2 %copy-start.9 = (bf16[2048,256]{1,0:T(8,128)(2,1)S(1)}, bf16[2048,256]{1,0:T(8,128)(2,1)}, u32[]{:S(2)}) copy-start(bf16[2048,256]{1,0:T(8,128)(2,1)} %copy-done.8) | copy-start | bytes 3145732
  23.6 9.2 %copy-start.11 = (bf16[2048,256]{1,0:T(8,128)(2,1)S(1)}, bf16[2048,256]{1,0:T(8,128)(2,1)}, u32[]{:S(2)}) copy-start(bf16[2048,256]{1,0:T(8,128)(2,1)} %copy-done.10) | copy-start | bytes 3145732
  35.8 22.2 %copy-start.20 = (bf16[256,512]{1,0:T(8,128)(2,1)S(1)}, bf16[256,512]{1,0:T(8,128)(2,1)}, u32[]{:S(2)}) copy-start(bf16[256,512]{1,0:T(8,128)(2,1)} %param.18) | copy-start | bytes 786436
  61.3 4.5 %collective-permute-start.2 = (bf16[2048,512]{0,1:T(8,128)(2,1)}, bf16[2048,512]{0,1:T(8,128)(2,1)}, u32[]{:S(2)}, u32[]{:S(2)}) collective-permute-start(bf16[2048,512]{0,1:T(8,128)(2,1)} %convolution_convert_fusion.1), channel_id=1, source_target_pairs={{0,1},{1,0},{2,3},{3,2},{4,5},{5,4},{6,7},{7,6},{8,9},{9,8},{10,11... | collective-permute-start | bytes 6291464 | tf_op jit(solution)/shard_map/ppermute | solution.py:239
  71.5 12.4 %copy-start.2 = (f32[2048,512]{0,1:T(8,128)}, f32[2048,512]{0,1:T(8,128)S(1)}, u32[]{:S(2)}) copy-start(f32[2048,512]{0,1:T(8,128)S(1)} %get-tuple-element.56) | copy-start | bytes 12582916
  83.8 7.1 %collective-permute-start.3 = (bf16[2048,512]{0,1:T(8,128)(2,1)}, bf16[2048,512]{0,1:T(8,128)(2,1)}, u32[]{:S(2)}, u32[]{:S(2)}) collective-permute-start(bf16[2048,512]{0,1:T(8,128)(2,1)} %convolution_convert_fusion), channel_id=1, source_target_pairs={{0,1},{1,0},{2,3},{3,2},{4,5},{5,4},{6,7},{7,6},{8,9},{9,8},{10,11... | collective-permute-start | bytes 6291464 | tf_op jit(solution)/shard_map/ppermute | solution.py:239
  90.8 249.0 %all-reduce.6.cloned.1.call-start = ((), (), s32[]{:S(2)}) async-start(), calls=%async_computation | async-start | bytes 2097152 | tf_op jit(solution)/shard_map/psum | solution.py:359
  90.8 5.1 %copy-start.3 = (f32[2048,512]{0,1:T(8,128)S(1)}, f32[2048,512]{0,1:T(8,128)}, u32[]{:S(2)}) copy-start(f32[2048,512]{0,1:T(8,128)} %copy-done.2) | copy-start | bytes 12582916
  90.9 5.3 %copy-start.7 = (bf16[2048,512]{0,1:T(8,128)(2,1)S(1)}, bf16[2048,512]{0,1:T(8,128)(2,1)}, u32[]{:S(2)}) copy-start(bf16[2048,512]{0,1:T(8,128)(2,1)} %copy.23) | copy-start | bytes 6291460
  104.3 35.5 %copy-start.31 = (f32[512]{0:T(512)S(1)}, f32[512]{0:T(512)}, u32[]{:S(2)}) copy-start(f32[512]{0:T(512)} %param.14) | copy-start | bytes 6148
  133.5 9.1 %copy-start.5 = (f32[2048,512]{0,1:T(8,128)S(1)}, f32[2048,512]{0,1:T(8,128)}, u32[]{:S(2)}) copy-start(f32[2048,512]{0,1:T(8,128)} %copy-done.4) | copy-start | bytes 12582916
  133.5 9.1 %copy-start.13 = (bf16[2048,256]{1,0:T(8,128)(2,1)S(1)}, bf16[2048,256]{1,0:T(8,128)(2,1)}, u32[]{:S(2)}) copy-start(bf16[2048,256]{1,0:T(8,128)(2,1)} %get-tuple-element.19) | copy-start | bytes 3145732
  134.8 16.1 %collective-permute-start.4 = (bf16[256,512]{1,0:T(8,128)(2,1)S(1)}, bf16[256,512]{1,0:T(8,128)(2,1)S(1)}, u32[]{:S(2)}, u32[]{:S(2)}) collective-permute-start(bf16[256,512]{1,0:T(8,128)(2,1)S(1)} %get-tuple-element.62), channel_id=1, source_target_pairs={{0,2},{2,4},{4,6},{6,8},{8,10},{10,12},{12,14},{14,16},{16,18},{18... | collective-permute-start | bytes 786440 | tf_op jit(solution)/shard_map/ppermute | solution.py:321
  138.6 13.1 %collective-permute-start.5 = (bf16[256,512]{1,0:T(8,128)(2,1)S(1)}, bf16[256,512]{1,0:T(8,128)(2,1)S(1)}, u32[]{:S(2)}, u32[]{:S(2)}) collective-permute-start(bf16[256,512]{1,0:T(8,128)(2,1)S(1)} %get-tuple-element.63), channel_id=1, source_target_pairs={{2,0},{4,2},{6,4},{8,6},{10,8},{12,10},{14,12},{16,14},{18,16},{20... | collective-permute-start | bytes 786440 | tf_op jit(solution)/shard_map/ppermute | solution.py:322
  142.7 9.0 %copy-start.19 = (f32[512,512]{1,0:T(8,128)S(1)}, f32[512,512]{1,0:T(8,128)}, u32[]{:S(2)}) copy-start(f32[512,512]{1,0:T(8,128)} %get-tuple-element.22) | copy-start | bytes 3145732
  144.2 7.7 %copy-start.23 = (bf16[512,256]{1,0:T(8,128)(2,1)S(1)}, bf16[512,256]{1,0:T(8,128)(2,1)}, u32[]{:S(2)}) copy-start(bf16[512,256]{1,0:T(8,128)(2,1)} %param.16) | copy-start | bytes 786436
  158.9 62.1 %copy-start.18 = (bf16[2048,256]{1,0:T(8,128)(2,1)S(1)}, bf16[2048,256]{1,0:T(8,128)(2,1)}, u32[]{:S(2)}) copy-start(bf16[2048,256]{1,0:T(8,128)(2,1)} %get-tuple-element.21) | copy-start | bytes 3145732
  158.9 62.1 %copy-start.27 = (bf16[512,256]{1,0:T(8,128)(2,1)S(1)}, bf16[512,256]{1,0:T(8,128)(2,1)}, u32[]{:S(2)}) copy-start(bf16[512,256]{1,0:T(8,128)(2,1)} %param.15) | copy-start | bytes 786436
  221.1 5.4 %copy-start.17 = (bf16[1024,512]{1,0:T(8,128)(2,1)S(1)}, bf16[1024,512]{1,0:T(8,128)(2,1)}, u32[]{:S(2)}) copy-start(bf16[1024,512]{1,0:T(8,128)(2,1)} %get-tuple-element.30) | copy-start | bytes 3145732
  226.5 120.6 %collective-permute-start.6 = (bf16[1024,512]{0,1:T(8,128)(2,1)}, bf16[1024,512]{0,1:T(8,128)(2,1)S(1)}, u32[]{:S(2)}, u32[]{:S(2)}) collective-permute-start(bf16[1024,512]{0,1:T(8,128)(2,1)} %constant_dynamic-slice_fusion), channel_id=1, source_target_pairs={{0,1},{1,0},{2,3},{3,2},{4,5},{5,4},{6,7},{7,6},{8,9},{9,8},{10,11... | collective-permute-start | bytes 3145736 | tf_op jit(solution)/shard_map/ppermute | solution.py:239
  229.7 120.5 %dynamic-slice-start = ((f32[2048]{0:T(1024)}, s32[]{:T(128)}), f32[1024]{0:T(1024)S(1)}, s32[]{:S(2)}) async-start(f32[2048]{0:T(1024)} %copy-done.28, s32[]{:T(128)} %select_n.20), calls=%async_computation.2 | async-start | bytes 8704 | tf_op jit(solution)/shard_map/dynamic-slice
  339.8 10.4 %copy-start.6 = (f32[2048,512]{0,1:T(8,128)S(1)}, f32[2048,512]{0,1:T(8,128)}, u32[]{:S(2)}) copy-start(f32[2048,512]{0,1:T(8,128)} %copy-done.4) | copy-start | bytes 12582916
  350.2 6.9 %copy-start.1 = (bf16[512,1024]{1,0:T(8,128)(2,1)S(1)}, bf16[512,1024]{1,0:T(8,128)(2,1)}, u32[]{:S(2)}) copy-start(bf16[512,1024]{1,0:T(8,128)(2,1)} %param.20) | copy-start | bytes 3145732
  (12 other events, 21.1 us)
Sparse Core Ops, SparseCore 0:
  90.9 130.0 all-reduce.7
  227.3 112.3 all-reduce.5

commit v2 on v1

--- a/solution.py
+++ b/solution.py
@@ -1,3 +1,4 @@
+import functools
 import math
 
 import jax
@@ -259,6 +260,100 @@
     return total
 
 
+def sum_kernel(
+    inner, scale, x_ref, out_ref, near, mid, far, gathered, near_sems, far_sems, back_sems, last_sems
+):
+    me = lax.axis_index("tm")
+    outer = x_ref.shape[1]
+    row = lax.div(me, inner)
+    col = lax.rem(me, inner)
+    near_peers = [row * inner + lax.rem(col + k, inner) for k in range(1, inner)]
+    far_peers = [lax.rem(row + k, outer) * inner + col for k in range(1, outer)]
+    barrier = pltpu.get_barrier_semaphore()
+    for peer in near_peers + far_peers:
+        pl.semaphore_signal(
+            barrier, inc=1, device_id={"tm": peer}, device_id_type=pl.DeviceIdType.MESH
+        )
+    pl.semaphore_wait(barrier, inner + outer - 2)
+
+    def send(source, target, sems, slot, peer):
+        copy = pltpu.make_async_remote_copy(
+            src_ref=source,
+            dst_ref=target,
+            send_sem=sems.at[0, slot],
+            recv_sem=sems.at[1, slot],
+            device_id={"tm": peer},
+            device_id_type=pl.DeviceIdType.MESH,
+        )
+        copy.start()
+        return copy
+
+    copies = [
+        send(x_ref.at[lax.rem(col + k, inner)], near.at[k - 1], near_sems, k - 1, near_peers[k - 1])
+        for k in range(1, inner)
+    ]
+    for copy in copies:
+        copy.wait()
+    total = x_ref[col].astype(jnp.float32)
+    for k in range(inner - 1):
+        total = total + near[k].astype(jnp.float32)
+    mid[...] = total.astype(jnp.bfloat16)
+    copies = [
+        send(mid.at[lax.rem(row + k, outer)], far.at[k - 1], far_sems, k - 1, far_peers[k - 1])
+        for k in range(1, outer)
+    ]
+    for copy in copies:
+        copy.wait()
+    total = mid[row].astype(jnp.float32)
+    for k in range(outer - 1):
+        total = total + far[k].astype(jnp.float32)
+    gathered[col, row] = total.astype(jnp.bfloat16)
+    copies = [
+        send(gathered.at[col, row], gathered.at[col, row], back_sems, k, far_peers[k])
+        for k in range(outer - 1)
+    ]
+    for copy in copies:
+        copy.wait()
+    copies = [
+        send(gathered.at[col], gathered.at[col], last_sems, k, near_peers[k])
+        for k in range(inner - 1)
+    ]
+    for copy in copies:
+        copy.wait()
+    out_ref[...] = gathered[...].astype(jnp.float32) * scale
+
+
+def slab_sum(stacked, scale):
+    count = lax.axis_size("tm")
+    inner = max(d for d in range(1, count + 1) if count % d == 0 and d * d <= count)
+    outer = count // inner
+    rows, cols = stacked.shape
+    piece = rows // count
+    low = jnp.bfloat16
+    total = pl.pallas_call(
+        functools.partial(sum_kernel, inner, scale),
+        out_shape=jax.ShapeDtypeStruct((inner, outer, piece, cols), jnp.float32),
+        in_specs=[pl.BlockSpec(memory_space=pltpu.VMEM)],
+        out_specs=pl.BlockSpec(memory_space=pltpu.VMEM),
+        scratch_shapes=[
+            pltpu.VMEM((inner - 1, outer, piece, cols), low),
+            pltpu.VMEM((outer, piece, cols), low),
+            pltpu.VMEM((outer - 1, piece, cols), low),
+            pltpu.VMEM((inner, outer, piece, cols), low),
+            pltpu.SemaphoreType.DMA((2, inner - 1)),
+            pltpu.SemaphoreType.DMA((2, outer - 1)),
+            pltpu.SemaphoreType.DMA((2, outer - 1)),
+            pltpu.SemaphoreType.DMA((2, inner - 1)),
+        ],
+        compiler_params=pltpu.CompilerParams(collective_id=0, has_side_effects=True),
+        cost_estimate=pl.CostEstimate(
+            flops=rows * cols * 4, bytes_accessed=rows * cols * 100, transcendentals=0
+        ),
+        name="slab_sum",
+    )(stacked.reshape(inner, outer, piece, cols))
+    return total.reshape(rows, cols)
+
+
 def local(
     frames,
     upstream,
@@ -350,15 +445,27 @@
     first_totals = lax.psum(
         (grad_inner_terms.astype(jnp.bfloat16), grad_outer_terms.astype(jnp.bfloat16)), "tm"
     )
-    attention_terms = tuple(
-        term.astype(jnp.bfloat16)
-        for term in (grad_query_terms, grad_key_terms, grad_value_terms, grad_out_terms)
-    )
-    attention_terms, first_totals = lax.optimization_barrier((attention_terms, first_totals))
-    totals = tuple(
-        total.astype(jnp.float32) for total in lax.psum(attention_terms, "tm") + first_totals
-    )
-    return (grad_frames,) + tuple((total * weight_scale for total in totals))
+    blocks = grad_out_terms.shape[1] // head_cols
+    stacked = jnp.concatenate(
+        [grad_query_terms, grad_key_terms, grad_value_terms]
+        + [grad_out_terms[:, i * head_cols : (i + 1) * head_cols] for i in range(blocks)],
+        axis=0,
+    ).astype(jnp.bfloat16)
+    summed = slab_sum(stacked, weight_scale)
+    depth = grad_query_terms.shape[0]
+    out_rows = grad_out_terms.shape[0]
+    grad_out = jnp.concatenate(
+        [summed[3 * depth + i * out_rows : 3 * depth + (i + 1) * out_rows] for i in range(blocks)],
+        axis=1,
+    )
+    first_totals, grad_out = lax.optimization_barrier((first_totals, grad_out))
+    return (
+        grad_frames,
+        summed[:depth],
+        summed[depth : 2 * depth],
+        summed[2 * depth : 3 * depth],
+        grad_out,
+    ) + tuple(total.astype(jnp.float32) * weight_scale for total in first_totals)
 
 
 def solution(mesh):

time: 368 us -> 249 us (0.68)
  waiting for transfers between devices: 184 us -> 23.3 us
  Pallas kernels: 51.4 us -> 104 us
  other arithmetic: 37.5 us -> 29.1 us
  matrix products: 45 us -> 37.1 us
  local copies, waits for them, and re-layouts: 18.9 us -> 23.9 us
    psum x1 -> x0, waiting for transfers between devices: 110 us -> none  [local(): lax.psum(attention_terms, 'tm') + first_totals]
    pallas_call x0 -> x1, Pallas kernels: none -> 53.1 us  [slab_sum(): pl.pallas_call(functools.partial(sum_kernel, inner, scale), out_shape=jax...]
    psum x1, waiting for transfers between devices: 60.6 us -> 9.01 us  [local(): lax.psum((grad_inner_terms.astype(jnp.bfloat16), grad_outer_terms.astype(...]
    mul x6 -> x2, other arithmetic: 10.5 us -> 4.96 us  [local(): total.astype(jnp.float32) * weight_scale]
    slice x0 -> x2, local copies, waits for them, and re-layouts: none -> 3.75 us  [the longest x1 2.68 us: local(): summed[2 * depth:3 * depth]]
    unnamed x71 -> x76, local copies, waits for them, and re-layouts: 13.7 us -> 14.2 us
  transfers between devices with their start and end apart: 9 -> 8, of which waited for: 7 -> 6; matrix products, arithmetic and copies ran while one was open for 16% -> 20% of each run, Pallas kernels for 8% -> 34%
where the time goes in v2:
time: 249 us; the launch traced here: 245 us
  Pallas kernels  104 us (42%)
  matrix products  37.1 us (15%)
  other arithmetic  29.1 us (12%)
  local copies, waits for them, and re-layouts  23.9 us (10%)
  waiting for transfers between devices  23.3 us (9%)
  between operations  14.9 us (6%)
  starting transfers between devices  12.1 us (5%)
    pallas_call x1, Pallas kernels, slab_sum(): pl.pallas_call(functools.partial(sum_kernel, inner, scale), out_shape=jax...  53.1 us
    pallas_call x1, Pallas kernels, attention_backward(): pl.pallas_call(backward_kernel, grid=(slab // rows,), in_specs=[pl.BlockS...  29.2 us
    pallas_call x1, Pallas kernels, attention_forward(): pl.pallas_call(forward_kernel, grid=(slab // rows,), in_specs=[pl.BlockSp...  22.2 us
    unnamed x76, local copies, waits for them, and re-layouts  14.2 us
    psum x1, waiting for transfers between devices, local(): lax.psum((grad_inner_terms.astype(jnp.bfloat16), grad_outer_terms.astype(...  9.01 us
    ppermute x1, waiting for transfers between devices, local(): lax.ppermute(sent_rim[HALF:], 'tm', [(i, i + 1) for i in range(count - 1)])  7.14 us
    reduce_sum x2, other arithmetic, layer_norm(): center = jnp.mean(inputs, axis=-1, keepdims=True)  6.04 us
    ppermute x1, starting transfers between devices, with_halo(): lax.ppermute(tail, axis, [(i, (i + 1) % count) for i in range(ends)])  5.58 us
  transfers between devices with their start and end apart: 8, of which 6 were waited for; matrix products, arithmetic and copies ran while one was open for 20% of the time, Pallas kernels for 34%

profile of v2, /device:TPU:0, one launch (start us, length us, event | category | flops | bytes accessed | tf_op | source)
XLA Modules:
  0.0 244.8 jit_solution(17710260543762077866)
XLA Ops:
  7.3 3.0 %copy.24 = bf16[2048,512]{0,1:T(8,128)(2,1)S(1)} copy(bf16[2048,512]{1,0:T(8,128)(2,1)} %param.11) | data formatting | bytes 4194304 | tf_op args[0]
  14.5 5.6 %collective-permute-start = (bf16[256,512]{1,0:T(8,128)(2,1)}, bf16[256,512]{1,0:T(8,128)(2,1)}, u32[]{:S(2)}, u32[]{:S(2)}) collective-permute-start(bf16[256,512]{1,0:T(8,128)(2,1)} %get-tuple-element.53), channel_id=1, source_target_pairs={{0,2},{2,4},{4,6},{6,8},{8,10},{10,12},{12,14},{14,16},{16,18},{18... | collective-permute-start | bytes 786440 | tf_op jit(solution)/shard_map/ppermute | solution.py:27
  22.3 2.0 reshape.89.record_key_ref
  24.3 2.7 %convolution_convert_fusion.5.query_ref = bf16[2048,256]{1,0:T(8,128)(2,1)} fusion(bf16[512,256]{1,0:T(8,128)(2,1)S(1)} %copy-done.28, f32[512]{0:T(512)} %param.14, f32[2048]{0:T(1024)S(1)} %add_rsqrt_fusion.1, f32[2048]{0:T(1024)S(1)} %broadcast_multiply_fusion.3, bf16[2048,512]{0,1:T(8,128)(2,1)S(1)} %copy.24), kind=kOutput, calls=%fused_computation.25 | convolution fusion | flops 542638080 | bytes 3426304 | tf_op jit(solution)/shard_map/dot_general | solution.py:51
  27.0 3.9 %collective-permute-done = bf16[256,512]{1,0:T(8,128)(2,1)} collective-permute-done((bf16[256,512]{1,0:T(8,128)(2,1)}, bf16[256,512]{1,0:T(8,128)(2,1)}, u32[]{:S(2)}, u32[]{:S(2)}) %collective-permute-start) | collective-permute-done | bytes 262176 | tf_op jit(solution)/shard_map/ppermute | solution.py:27
  30.9 1.9 collective-permute-done.1
  32.8 3.0 %pad_maximum_fusion.pair_ref = bf16[2560,512]{1,0:T(8,128)(2,1)} fusion(bf16[256,512]{1,0:T(8,128)(2,1)} %collective-permute-done.1, bf16[2048,256]{1,0:T(8,128)(2,1)S(1)} %copy-done.14, bf16[2048,256]{1,0:T(8,128)(2,1)S(1)} %copy-done.12, bf16[256,512]{1,0:T(8,128)(2,1)} %collective-permute-done), kind=kLoop, calls=%fused_computation.21 | loop fusion | flops 10485760 | bytes 5242880 | tf_op jit(solution)/shard_map/concatenate | solution.py:25
  35.8 22.2 %attention_forward.1 = (bf16[2048,256]{1,0:T(8,128)(2,1)}, f32[4,2048]{1,0:T(4,128)}) custom-call(bf16[2048,256]{1,0:T(8,128)(2,1)} %convolution_convert_fusion.5.query_ref, bf16[2560,512]{1,0:T(8,128)(2,1)} %pad_maximum_fusion.pair_ref, s32[1,2048]{1,0:T(1,128)} %bitcast.29, s32[2560,1]{1,0:T(8,128)} %reshape.89.record_key_ref), custom_call_target="tpu_custom_call" | custom-call | flops 6442450944 | bytes 4194304 | tf_op jit(solution)/shard_map/attention_forward/pallas_call | solution.py:175
  58.0 3.3 %convolution_convert_fusion.1 = bf16[2048,512]{0,1:T(8,128)(2,1)} fusion(bf16[2048,256]{1,0:T(8,128)(2,1)} %get-tuple-element.16, bf16[256,512]{1,0:T(8,128)(2,1)S(1)} %copy-done.22), kind=kOutput, calls=%fused_computation.20 | convolution fusion | flops 537919488 | bytes 3407872 | tf_op jit(solution)/shard_map/dot_general | solution.py:390
  61.3 3.9 %copy.23 = bf16[2048,512]{0,1:T(8,128)(2,1)} copy(bf16[2048,512]{1,0:T(8,128)(2,1)} %param.12) | data formatting | bytes 4194304 | tf_op args[1]
  65.8 5.7 %fusion.19 = (f32[2048]{0:T(1024)S(1)}, f32[2048,512]{0,1:T(8,128)S(1)}, f32[2048,512]{0,1:T(8,128)}) fusion(bf16[2048,512]{0,1:T(8,128)(2,1)} %collective-permute-done.2, bf16[2048,512]{0,1:T(8,128)(2,1)} %convolution_convert_fusion.1, bf16[2048,512]{0,1:T(8,128)(2,1)S(1)} %copy.24, f32[2048]{0:T(1024)S(1)} %add_rsqrt_fusion.1, ...), kind=kLoop, calls=%fused_computation.70 | loop fusion | flops 8386560 | bytes 14704640 | tf_op jit(solution)/shard_map/reduce_sum | solution.py:37
  72.1 2.5 %fusion.18 = f32[2048,1024]{1,0:T(8,128)S(1)} fusion(bf16[512,1024]{1,0:T(8,128)(2,1)S(1)} %copy-done, f32[2048,512]{0,1:T(8,128)S(1)} %get-tuple-element.46, f32[512]{0:T(512)S(1)} %copy-done.34, f32[2048]{0:T(1024)S(1)} %add_rsqrt_fusion, f32[2048]{0:T(1024)S(1)} %broadcast_multiply_fusion.2), kind=kOutput, calls=%fused_computation.69 | convolution fusion | flops 2151677952 | bytes 13649920 | tf_op jit(solution)/shard_map/dot_general | solution.py:394
  74.8 5.3 %multiply_convert_fusion.1 = bf16[2048,1024]{1,0:T(8,128)(2,1)S(1)} fusion(f32[2048,1024]{1,0:T(8,128)S(1)} %fusion.18, bf16[2048,512]{1,0:T(8,128)(2,1)S(1)} %copy-done.17, bf16[1024,512]{1,0:T(8,128)(2,1)S(1)} %copy-done.35), kind=kOutput, calls=%fused_computation.1 | convolution fusion | flops 2168455168 | bytes 15728640 | tf_op jit(solution)/shard_map/dot_general | solution.py:397
  80.0 3.7 %convolution_convert_fusion = bf16[2048,512]{0,1:T(8,128)(2,1)} fusion(bf16[2048,1024]{1,0:T(8,128)(2,1)S(1)} %multiply_convert_fusion.1, bf16[512,1024]{1,0:T(8,128)(2,1)S(1)} %copy-done), kind=kOutput, calls=%fused_computation.19 | convolution fusion | flops 2148532224 | bytes 7340032 | tf_op jit(solution)/shard_map/dot_general | solution.py:403
  83.9 3.4 %convolution_convert_fusion.6 = bf16[512,1024]{1,0:T(8,128)(2,1)} fusion(bf16[2048,1024]{1,0:T(8,128)(2,1)S(1)} %multiply_convert_fusion.1, f32[2048,512]{0,1:T(8,128)S(1)} %get-tuple-element.46, f32[512]{0:T(512)S(1)} %copy-done.34, f32[2048]{0:T(1024)S(1)} %add_rsqrt_fusion, f32[2048]{0:T(1024)S(1)} %broadcast_multiply_fusion.2), kind=kOutput, calls=%fused_computation.34 | convolution fusion | flops 2152202240 | bytes 9455616 | tf_op jit(solution)/shard_map/dot_general | solution.py:402
  87.3 3.5 %multiply_convert_fusion.5 = bf16[1024,512]{1,0:T(8,128)(2,1)} fusion(bf16[2048,512]{1,0:T(8,128)(2,1)S(1)} %copy-done.17, f32[2048,1024]{1,0:T(8,128)S(1)} %fusion.18), kind=kOutput, calls=%fused_computation.29 | convolution fusion | flops 2159017984 | bytes 11534336 | tf_op jit(solution)/shard_map/dot_general | solution.py:401
  90.8 5.0 %fusion.4 = (f32[2048]{0:T(1024)S(1)}, f32[2048]{0:T(1024)S(1)}) fusion(bf16[2048,512]{0,1:T(8,128)(2,1)} %collective-permute-done.3, bf16[2048,512]{0,1:T(8,128)(2,1)} %convolution_convert_fusion, f32[512]{0:T(512)S(1)} %copy-done.34, f32[2048]{0:T(1024)S(1)} %add_rsqrt_fusion, f32[2048,512]{0,1:T(8,128)} %copy-done.2, f32[2048]{0:T(1024)S(1)} %broadcast_multiply_fusion.2), kind=kLoop, calls=%fused_computation.18 | loop fusion | flops 9433088 | bytes 8423424 | tf_op jit(solution)/shard_map/reduce_sum | solution.py:45
  96.1 4.4 %multiply_add_fusion = f32[2048,512]{0,1:T(8,128)S(1)} fusion(bf16[2048,512]{0,1:T(8,128)(2,1)S(1)} %copy-done.10, f32[2048,512]{0,1:T(8,128)S(1)} %copy-done.3, bf16[2048,512]{0,1:T(8,128)(2,1)} %collective-permute-done.3, bf16[2048,512]{0,1:T(8,128)(2,1)} %convolution_convert_fusion, f32[2048]{0:T(1024)S(1)} %get-tuple-element.59, ...), kind=kLoop, calls=%fused_computation.10 | loop fusion | flops 12582912 | bytes 14714880 | tf_op jit(solution)/shard_map/add | solution.py:405
  100.6 2.0 copy-done.4
  102.6 1.7 convolution_convert_fusion.2.grad_ref
  104.3 29.2 %attention_backward.1 = (bf16[2048,256]{1,0:T(8,128)(2,1)}, bf16[2048,512]{1,0:T(8,128)(2,1)}, f32[512,512]{1,0:T(8,128)}, bf16[512,512]{1,0:T(8,128)(2,1)}) custom-call(bf16[2048,256]{1,0:T(8,128)(2,1)} %convolution_convert_fusion.5.query_ref, bf16[2560,512]{1,0:T(8,128)(2,1)} %pad_maximum_fusion.pair_ref, ...), custom_call_target="tpu_custom_call" | custom-call | flops 16106127360 | bytes 8388608 | tf_op jit(solution)/shard_map/attention_backward/pallas_call | solution.py:205
  134.8 3.6 %collective-permute-start.4 = (bf16[256,512]{1,0:T(8,128)(2,1)S(1)}, bf16[256,512]{1,0:T(8,128)(2,1)S(1)}, u32[]{:S(2)}, u32[]{:S(2)}) collective-permute-start(bf16[256,512]{1,0:T(8,128)(2,1)S(1)} %get-tuple-element.57), channel_id=1, source_target_pairs={{0,2},{2,4},{4,6},{6,8},{8,10},{10,12},{12,14},{14,16},{16,18},{18... | collective-permute-start | bytes 786440 | tf_op jit(solution)/shard_map/ppermute | solution.py:416
  139.7 3.0 %fusion.6 = bf16[2048,256]{1,0:T(8,128)(2,1)} fusion(bf16[2048,256]{1,0:T(8,128)(2,1)} %get-tuple-element.18, f32[512]{0:T(512)S(1)} %copy-done.33, f32[2048]{0:T(1024)S(1)} %add_rsqrt_fusion.1, f32[2048]{0:T(1024)S(1)} %broadcast_multiply_fusion.3, bf16[2048,512]{0,1:T(8,128)(2,1)S(1)} %copy.24), kind=kOutput, calls=%fused_computation.39 | convolution fusion | flops 542244864 | bytes 3426304 | tf_op jit(solution)/shard_map/dot_general | solution.py:428
  143.6 7.1 %collective-permute-done.4 = bf16[256,512]{1,0:T(8,128)(2,1)S(1)} collective-permute-done((bf16[256,512]{1,0:T(8,128)(2,1)S(1)}, bf16[256,512]{1,0:T(8,128)(2,1)S(1)}, u32[]{:S(2)}, u32[]{:S(2)}) %collective-permute-start.4) | collective-permute-done | bytes 262176 | tf_op jit(solution)/shard_map/ppermute | solution.py:416
  157.5 1.5 fusion.8
  160.4 53.1 %slab_sum.1 = f32[4,4,128,256]{3,2,1,0:T(8,128)} custom-call(bf16[4,4,128,256]{3,2,1,0:T(8,128)(2,1)} %bitcast.1.x_ref), custom_call_target="tpu_custom_call" | custom-call | flops 2097152 | bytes 52428800 | tf_op jit(solution)/shard_map/slab_sum/pallas_call | solution.py:333
  215.4 9.0 %all-reduce.4.cloned.1.call-done = (bf16[512,1024]{1,0:T(8,128)(2,1)}, bf16[1024,512]{1,0:T(8,128)(2,1)}) async-done(((bf16[512,1024]{1,0:T(8,128)(2,1)}, bf16[1024,512]{1,0:T(8,128)(2,1)}), (bf16[512,1024]{1,0:T(8,128)(2,1)}, bf16[1024,512]{1,0:T(8,128)(2,1)})) %all-reduce.4.cloned.1.call-update) | async-done | bytes 2097168 | tf_op jit(solution)/shard_map/psum | solution.py:445
  224.4 2.7 %fusion.21 = (f32[1,4,128,256]{3,2,1,0:T(8,128)}, f32[1,4,128,256]{3,2,1,0:T(8,128)}, f32[1,4,128,256]{3,2,1,0:T(8,128)}) fusion(f32[4,4,128,256]{3,2,1,0:T(8,128)} %slab_sum.1), kind=kLoop, calls=%fused_computation.72 | loop fusion | bytes 3145728 | tf_op jit(solution)/shard_map/slice | solution.py:466
  227.1 3.3 %convert_multiply_fusion.1 = f32[512,1024]{1,0:T(8,128)} fusion(bf16[512,1024]{1,0:T(8,128)(2,1)} %get-tuple-element.23), kind=kLoop, calls=%fused_computation.28 | loop fusion | flops 1048576 | bytes 3145728 | tf_op jit(solution)/shard_map/mul | solution.py:468
  230.4 1.6 convert_multiply_fusion
  233.8 2.0 multiply_add_fusion.1
  235.7 1.8 copy.29
  (114 shorter events, 23.3 us)
Async XLA Ops:
  7.2 64.8 %copy-start = (bf16[512,1024]{1,0:T(8,128)(2,1)S(1)}, bf16[512,1024]{1,0:T(8,128)(2,1)}, u32[]{:S(2)}) copy-start(bf16[512,1024]{1,0:T(8,128)(2,1)} %param.20) | copy-start | bytes 3145732
  7.2 4.1 %copy-start.31 = (f32[512]{0:T(512)S(1)}, f32[512]{0:T(512)}, u32[]{:S(2)}) copy-start(f32[512]{0:T(512)} %param.14) | copy-start | bytes 6148
  7.2 4.1 %copy-start.26 = (bf16[512,256]{1,0:T(8,128)(2,1)S(1)}, bf16[512,256]{1,0:T(8,128)(2,1)}, u32[]{:S(2)}) copy-start(bf16[512,256]{1,0:T(8,128)(2,1)} %param.16) | copy-start | bytes 786436
  7.2 217.2 %all-reduce.4.cloned.1.call-start = ((), (), s32[]{:S(2)}) async-start(), calls=%async_computation | async-start | bytes 4194304 | tf_op jit(solution)/shard_map/psum | solution.py:445
  11.3 146.3 %copy-start.30 = (f32[2048]{0:T(1024)}, f32[2048]{0:T(1024)S(1)}, u32[]{:S(2)}) copy-start(f32[2048]{0:T(1024)S(1)} %add_rsqrt_fusion.1) | copy-start | bytes 24580
  12.3 9.2 %copy-start.23 = (s32[32768]{0:T(1024)S(1)}, s32[32768]{0:T(1024)}, u32[]{:S(2)}) copy-start(s32[32768]{0:T(1024)} %param.13) | copy-start | bytes 393220
  12.3 11.9 %copy-start.28 = (bf16[512,256]{1,0:T(8,128)(2,1)S(1)}, bf16[512,256]{1,0:T(8,128)(2,1)}, u32[]{:S(2)}) copy-start(bf16[512,256]{1,0:T(8,128)(2,1)} %param.15) | copy-start | bytes 786436
  14.5 16.4 %collective-permute-start = (bf16[256,512]{1,0:T(8,128)(2,1)}, bf16[256,512]{1,0:T(8,128)(2,1)}, u32[]{:S(2)}, u32[]{:S(2)}) collective-permute-start(bf16[256,512]{1,0:T(8,128)(2,1)} %get-tuple-element.53), channel_id=1, source_target_pairs={{0,2},{2,4},{4,6},{6,8},{8,10},{10,12},{12,14},{14,16},{16,18},{18... | collective-permute-start | bytes 786440 | tf_op jit(solution)/shard_map/ppermute | solution.py:27
  20.1 12.7 %collective-permute-start.1 = (bf16[256,512]{1,0:T(8,128)(2,1)}, bf16[256,512]{1,0:T(8,128)(2,1)}, u32[]{:S(2)}, u32[]{:S(2)}) collective-permute-start(bf16[256,512]{1,0:T(8,128)(2,1)} %get-tuple-element.54), channel_id=1, source_target_pairs={{2,0},{4,2},{6,4},{8,6},{10,8},{12,10},{14,12},{16,14},{18,16},{20... | collective-permute-start | bytes 786440 | tf_op jit(solution)/shard_map/ppermute | solution.py:29
  22.3 10.5 %copy-start.12 = (bf16[2048,256]{1,0:T(8,128)(2,1)S(1)}, bf16[2048,256]{1,0:T(8,128)(2,1)}, u32[]{:S(2)}) copy-start(bf16[2048,256]{1,0:T(8,128)(2,1)} %copy-done.11) | copy-start | bytes 3145732
  22.3 10.5 %copy-start.14 = (bf16[2048,256]{1,0:T(8,128)(2,1)S(1)}, bf16[2048,256]{1,0:T(8,128)(2,1)}, u32[]{:S(2)}) copy-start(bf16[2048,256]{1,0:T(8,128)(2,1)} %copy-done.13) | copy-start | bytes 3145732
  35.8 22.2 %copy-start.22 = (bf16[256,512]{1,0:T(8,128)(2,1)S(1)}, bf16[256,512]{1,0:T(8,128)(2,1)}, u32[]{:S(2)}) copy-start(bf16[256,512]{1,0:T(8,128)(2,1)} %param.18) | copy-start | bytes 786436
  61.3 4.5 %collective-permute-start.2 = (bf16[2048,512]{0,1:T(8,128)(2,1)}, bf16[2048,512]{0,1:T(8,128)(2,1)}, u32[]{:S(2)}, u32[]{:S(2)}) collective-permute-start(bf16[2048,512]{0,1:T(8,128)(2,1)} %convolution_convert_fusion.1), channel_id=1, source_target_pairs={{0,1},{1,0},{2,3},{3,2},{4,5},{5,4},{6,7},{7,6},{8,9},{9,8},{10,11... | collective-permute-start | bytes 6291464 | tf_op jit(solution)/shard_map/ppermute | solution.py:240
  71.4 12.4 %copy-start.2 = (f32[2048,512]{0,1:T(8,128)}, f32[2048,512]{0,1:T(8,128)S(1)}, u32[]{:S(2)}) copy-start(f32[2048,512]{0,1:T(8,128)S(1)} %get-tuple-element.46) | copy-start | bytes 12582916
  83.7 7.1 %collective-permute-start.3 = (bf16[2048,512]{0,1:T(8,128)(2,1)}, bf16[2048,512]{0,1:T(8,128)(2,1)}, u32[]{:S(2)}, u32[]{:S(2)}) collective-permute-start(bf16[2048,512]{0,1:T(8,128)(2,1)} %convolution_convert_fusion), channel_id=1, source_target_pairs={{0,1},{1,0},{2,3},{3,2},{4,5},{5,4},{6,7},{7,6},{8,9},{9,8},{10,11... | collective-permute-start | bytes 6291464 | tf_op jit(solution)/shard_map/ppermute | solution.py:240
  90.8 5.1 %copy-start.3 = (f32[2048,512]{0,1:T(8,128)S(1)}, f32[2048,512]{0,1:T(8,128)}, u32[]{:S(2)}) copy-start(f32[2048,512]{0,1:T(8,128)} %copy-done.2) | copy-start | bytes 12582916
  90.8 5.3 %copy-start.10 = (bf16[2048,512]{0,1:T(8,128)(2,1)S(1)}, bf16[2048,512]{0,1:T(8,128)(2,1)}, u32[]{:S(2)}) copy-start(bf16[2048,512]{0,1:T(8,128)(2,1)} %copy.23) | copy-start | bytes 6291460
  104.3 35.3 %copy-start.33 = (f32[512]{0:T(512)S(1)}, f32[512]{0:T(512)}, u32[]{:S(2)}) copy-start(f32[512]{0:T(512)} %param.14) | copy-start | bytes 6148
  133.5 9.1 %copy-start.18 = (bf16[2048,512]{1,0:T(8,128)(2,1)S(1)}, bf16[2048,512]{1,0:T(8,128)(2,1)}, u32[]{:S(2)}) copy-start(bf16[2048,512]{1,0:T(8,128)(2,1)} %get-tuple-element.21) | copy-start | bytes 6291460
  134.8 16.0 %collective-permute-start.4 = (bf16[256,512]{1,0:T(8,128)(2,1)S(1)}, bf16[256,512]{1,0:T(8,128)(2,1)S(1)}, u32[]{:S(2)}, u32[]{:S(2)}) collective-permute-start(bf16[256,512]{1,0:T(8,128)(2,1)S(1)} %get-tuple-element.57), channel_id=1, source_target_pairs={{0,2},{2,4},{4,6},{6,8},{8,10},{10,12},{12,14},{14,16},{16,18},{18... | collective-permute-start | bytes 786440 | tf_op jit(solution)/shard_map/ppermute | solution.py:416
  138.4 13.1 %collective-permute-start.5 = (bf16[256,512]{1,0:T(8,128)(2,1)S(1)}, bf16[256,512]{1,0:T(8,128)(2,1)S(1)}, u32[]{:S(2)}, u32[]{:S(2)}) collective-permute-start(bf16[256,512]{1,0:T(8,128)(2,1)S(1)} %get-tuple-element.58), channel_id=1, source_target_pairs={{2,0},{4,2},{6,4},{8,6},{10,8},{12,10},{14,12},{16,14},{18,16},{20... | collective-permute-start | bytes 786440 | tf_op jit(solution)/shard_map/ppermute | solution.py:417
  139.7 3.1 %copy-start.5 = (f32[2048,512]{0,1:T(8,128)S(1)}, f32[2048,512]{0,1:T(8,128)}, u32[]{:S(2)}) copy-start(f32[2048,512]{0,1:T(8,128)} %copy-done.4) | copy-start | bytes 12582916
  139.7 3.1 %copy-start.16 = (bf16[2048,256]{1,0:T(8,128)(2,1)S(1)}, bf16[2048,256]{1,0:T(8,128)(2,1)}, u32[]{:S(2)}) copy-start(bf16[2048,256]{1,0:T(8,128)(2,1)} %get-tuple-element.16) | copy-start | bytes 3145732
  142.6 8.8 %copy-start.21 = (f32[512,512]{1,0:T(8,128)S(1)}, f32[512,512]{1,0:T(8,128)}, u32[]{:S(2)}) copy-start(f32[512,512]{1,0:T(8,128)} %get-tuple-element.19) | copy-start | bytes 3145732
  143.6 8.2 %copy-start.25 = (bf16[512,256]{1,0:T(8,128)(2,1)S(1)}, bf16[512,256]{1,0:T(8,128)(2,1)}, u32[]{:S(2)}) copy-start(bf16[512,256]{1,0:T(8,128)(2,1)} %param.17) | copy-start | bytes 786436
  156.0 76.1 %collective-permute-start.6 = (bf16[1024,512]{0,1:T(8,128)(2,1)}, bf16[1024,512]{0,1:T(8,128)(2,1)S(1)}, u32[]{:S(2)}, u32[]{:S(2)}) collective-permute-start(bf16[1024,512]{0,1:T(8,128)(2,1)} %constant_dynamic-slice_fusion), channel_id=1, source_target_pairs={{0,1},{1,0},{2,3},{3,2},{4,5},{5,4},{6,7},{7,6},{8,9},{9,8},{10,11... | collective-permute-start | bytes 3145736 | tf_op jit(solution)/shard_map/ppermute | solution.py:240
  224.4 6.0 %copy-start.19 = (bf16[1024,512]{1,0:T(8,128)(2,1)S(1)}, bf16[1024,512]{1,0:T(8,128)(2,1)}, u32[]{:S(2)}) copy-start(bf16[1024,512]{1,0:T(8,128)(2,1)} %get-tuple-element.24) | copy-start | bytes 3145732
  224.4 7.7 %copy-start.7 = (f32[2048,512]{0,1:T(8,128)S(1)}, f32[2048,512]{0,1:T(8,128)}, u32[]{:S(2)}) copy-start(f32[2048,512]{0,1:T(8,128)} %get-tuple-element.52) | copy-start | bytes 12582916
  224.4 7.7 %copy-start.9 = (bf16[2048,512]{0,1:T(8,128)(2,1)S(1)}, bf16[2048,512]{0,1:T(8,128)(2,1)}, u32[]{:S(2)}) copy-start(bf16[2048,512]{0,1:T(8,128)(2,1)} %copy-done.8) | copy-start | bytes 6291460
  230.4 3.3 %copy-start.6 = (f32[2048,512]{0,1:T(8,128)S(1)}, f32[2048,512]{0,1:T(8,128)}, u32[]{:S(2)}) copy-start(f32[2048,512]{0,1:T(8,128)} %copy-done.4) | copy-start | bytes 12582916
  230.4 3.3 %dynamic-slice-start = ((f32[2048]{0:T(1024)}, s32[]{:T(128)}), f32[1024]{0:T(1024)S(1)}, s32[]{:S(2)}) async-start(f32[2048]{0:T(1024)} %copy-done.30, s32[]{:T(128)} %select_n.20), calls=%async_computation.1 | async-start | bytes 8704 | tf_op jit(solution)/shard_map/dynamic-slice
  233.8 3.8 %copy-start.1 = (bf16[512,1024]{1,0:T(8,128)(2,1)S(1)}, bf16[512,1024]{1,0:T(8,128)(2,1)}, u32[]{:S(2)}) copy-start(bf16[512,1024]{1,0:T(8,128)(2,1)} %param.20) | copy-start | bytes 3145732
  (13 other events, 20.3 us)
Sparse Core Ops, SparseCore 0:
  90.9 133.4 all-reduce.3

commit v3 on v2

--- a/solution.py
+++ b/solution.py
@@ -71,7 +71,9 @@
     return jnp.where(own, value, 0.0).astype(jnp.bfloat16)
 
 
-def forward_kernel(query_ref, pair_ref, record_query_ref, record_key_ref, context_ref, lse_ref):
+def forward_kernel(
+    query_ref, pair_ref, record_query_ref, record_key_ref, weight_ref, context_ref, lse_ref, term_ref
+):
     rows, cols = query_ref.shape
     window = rows + 2 * HALF
     start = pl.multiple_of(pl.program_id(0) * rows, rows)
@@ -97,6 +99,7 @@
             parts.append(mixed * (1.0 / total))
             lse_ref[2 * pair + head : 2 * pair + head + 1, :] = peak + jnp.log(total)
         context_ref[:, lanes] = jnp.concatenate(parts, axis=0).T.astype(jnp.bfloat16)
+    term_ref[...] = contract(context_ref[...], weight_ref[...], ((1,), (0,))).astype(jnp.bfloat16)
 
 
 def backward_kernel(
@@ -168,7 +171,7 @@
     return pl.BlockSpec(shape, lambda i: (0, 0))
 
 
-def attention_forward(queries, pairs, record_query, record_key):
+def attention_forward(queries, pairs, record_query, record_key, weight):
     slab, cols = queries.shape
     heads = cols // HEAD_DIM
     rows = HALF
@@ -180,14 +183,17 @@
             whole(pairs.shape),
             pl.BlockSpec((1, rows), lambda i: (0, i)),
             whole(record_key.shape),
+            whole(weight.shape),
         ],
         out_specs=[
             pl.BlockSpec((rows, cols), lambda i: (i, 0)),
             pl.BlockSpec((heads, rows), lambda i: (0, i)),
+            pl.BlockSpec((rows, weight.shape[1]), lambda i: (i, 0)),
         ],
         out_shape=[
             jax.ShapeDtypeStruct((slab, cols), jnp.bfloat16),
             jax.ShapeDtypeStruct((heads, slab), jnp.float32),
+            jax.ShapeDtypeStruct((slab, weight.shape[1]), jnp.bfloat16),
         ],
         cost_estimate=pl.CostEstimate(
             flops=4 * slab * 3 * HALF * cols * 4,
@@ -195,7 +201,7 @@
             transcendentals=slab * 3 * HALF * heads,
         ),
         name="attention_forward",
-    )(queries, pairs, record_query, record_key)
+    )(queries, pairs, record_query, record_key, weight)
 
 
 def attention_backward(queries, pairs, grad_context, lse, record_query, record_key):
@@ -386,8 +392,9 @@
     key_value_ext = with_halo(key_value, (("tm", 0),), HALF)
     record_query = record_ext[HALF : HALF + slab_rows].reshape(1, slab_rows)
     record_key = record_ext.reshape(slab_rows + 2 * HALF, 1)
-    context, lse = attention_forward(queries, key_value_ext, record_query, record_key)
-    partial_value = jnp.dot(context, out_weight, preferred_element_type=jnp.float32)
+    context, lse, partial_value = attention_forward(
+        queries, key_value_ext, record_query, record_key, out_weight
+    )
     middle = frames_wide + group_sum(partial_value)
     scaled_second, inverse_second = layer_norm(middle)
     normed_second = (scaled_second * second_gain).astype(jnp.bfloat16)

time: 249 us -> 244 us (0.980); the launches traced: 245 us -> 243 us
  waiting for transfers between devices: 23.3 us -> 38.7 us
  local copies, waits for them, and re-layouts: 23.9 us -> 14.2 us
  matrix products: 37.1 us -> 31.2 us
  Pallas kernels: 104 us -> 100 us
  other arithmetic: 29.1 us -> 32.4 us
    psum x1, waiting for transfers between devices: 9.01 us -> 20.1 us  [local(): lax.psum((grad_inner_terms.astype(jnp.bfloat16), grad_outer_terms.astype(...]
    unnamed x76 -> x67, local copies, waits for them, and re-layouts: 14.2 us -> 3.25 us
    pallas_call x1, Pallas kernels: 53.1 us -> 47.3 us  [slab_sum(): pl.pallas_call(functools.partial(sum_kernel, inner, scale), out_shape=jax...]
    ppermute x3, waiting for transfers between devices: 0.59 us -> 4.5 us  [shift(): lax.ppermute(array, axis, [(i, (i + by) % count) for i in range(count)])]
    dot_general x1 -> x0, matrix products: 3.3 us -> none  [local(): jnp.dot(context, out_weight, preferred_element_type=jnp.float32)]
  transfers between devices with their start and end apart: 8 -> 8, of which waited for: 6 -> 6; matrix products, arithmetic and copies ran while one was open for 20% -> 18% of each run, Pallas kernels for 34% -> 31%
where the time goes in v3:
time: 244 us; the launch traced here: 243 us
  Pallas kernels  100 us (41%)
  waiting for transfers between devices  38.7 us (16%)
  other arithmetic  32.4 us (13%)
  matrix products  31.2 us (13%)
  between operations  14.6 us (6%)
  local copies, waits for them, and re-layouts  14.2 us (6%)
  starting transfers between devices  12.1 us (5%)
    pallas_call x1, Pallas kernels, slab_sum(): pl.pallas_call(functools.partial(sum_kernel, inner, scale), out_shape=jax...  47.3 us
    pallas_call x1, Pallas kernels, attention_backward(): pl.pallas_call(backward_kernel, grid=(slab // rows,), in_specs=[pl.BlockS...  29.2 us
    pallas_call x1, Pallas kernels, attention_forward(): pl.pallas_call(forward_kernel, grid=(slab // rows,), in_specs=[pl.BlockSp...  23.7 us
    psum x1, waiting for transfers between devices, local(): lax.psum((grad_inner_terms.astype(jnp.bfloat16), grad_outer_terms.astype(...  20.1 us
    ppermute x1, waiting for transfers between devices, local(): lax.ppermute(sent_rim[HALF:], 'tm', [(i, i + 1) for i in range(count - 1)])  8.09 us
    ppermute x1, starting transfers between devices, with_halo(): lax.ppermute(tail, axis, [(i, (i + 1) % count) for i in range(ends)])  5.58 us
    dot_general x1, matrix products, local(): jnp.dot(upstream, outer_weight.T, preferred_element_type=jnp.float32) * 0.5  5.48 us
    reduce_sum x2, other arithmetic, layer_norm(): center = jnp.mean(inputs, axis=-1, keepdims=True)  5.2 us
  transfers between devices with their start and end apart: 8, of which 6 were waited for; matrix products, arithmetic and copies ran while one was open for 18% of the time, Pallas kernels for 31%

profile of v3, /device:TPU:0, one launch (start us, length us, event | category | flops | bytes accessed | tf_op | source)
XLA Modules:
  0.0 243.4 jit_solution(9662208445974358079)
XLA Ops:
  7.3 2.1 convert_reduce_fusion
  9.4 2.5 %fusion.2 = f32[2048]{0:T(1024)S(1)} fusion(bf16[2048,512]{1,0:T(8,128)(2,1)} %param.11, f32[2048]{0:T(1024)S(1)} %broadcast_multiply_fusion.3), kind=kLoop, calls=%fused_computation.8 | loop fusion | flops 4192256 | bytes 2113536 | tf_op jit(solution)/shard_map/reduce_sum | solution.py:39
  11.9 2.4 fusion
  17.3 5.6 %collective-permute-start = (bf16[256,512]{1,0:T(8,128)(2,1)}, bf16[256,512]{1,0:T(8,128)(2,1)}, u32[]{:S(2)}, u32[]{:S(2)}) collective-permute-start(bf16[256,512]{1,0:T(8,128)(2,1)} %get-tuple-element.42), channel_id=1, source_target_pairs={{0,2},{2,4},{4,6},{6,8},{8,10},{10,12},{12,14},{14,16},{16,18},{18... | collective-permute-start | bytes 786440 | tf_op jit(solution)/shard_map/ppermute | solution.py:27
  22.9 1.5 collective-permute-start.1
  25.2 2.0 reshape.89.record_key_ref
  27.1 3.3 %convolution_convert_fusion.4.query_ref = bf16[2048,256]{1,0:T(8,128)(2,1)} fusion(bf16[2048,512]{1,0:T(8,128)(2,1)} %copy-done.8, bf16[512,256]{1,0:T(8,128)(2,1)S(1)} %copy-done.22), kind=kOutput, calls=%fused_computation.24 | convolution fusion | flops 537395200 | bytes 3407872 | tf_op jit(solution)/shard_map/dot_general | solution.py:51
  30.4 3.3 %collective-permute-done = bf16[256,512]{1,0:T(8,128)(2,1)} collective-permute-done((bf16[256,512]{1,0:T(8,128)(2,1)}, bf16[256,512]{1,0:T(8,128)(2,1)}, u32[]{:S(2)}, u32[]{:S(2)}) %collective-permute-start) | collective-permute-done | bytes 262176 | tf_op jit(solution)/shard_map/ppermute | solution.py:27
  33.7 1.9 collective-permute-done.1
  35.6 3.0 %pad_maximum_fusion.pair_ref = bf16[2560,512]{1,0:T(8,128)(2,1)} fusion(bf16[256,512]{1,0:T(8,128)(2,1)} %collective-permute-done.1, bf16[2048,256]{1,0:T(8,128)(2,1)S(1)} %copy-done.11, bf16[2048,256]{1,0:T(8,128)(2,1)S(1)} %copy-done.13, bf16[256,512]{1,0:T(8,128)(2,1)} %collective-permute-done), kind=kLoop, calls=%fused_computation.20 | loop fusion | flops 10485760 | bytes 5242880 | tf_op jit(solution)/shard_map/concatenate | solution.py:25
  38.6 23.7 %attention_forward.1 = (bf16[2048,256]{1,0:T(8,128)(2,1)}, f32[4,2048]{1,0:T(4,128)}, bf16[2048,512]{1,0:T(8,128)(2,1)}) custom-call(bf16[2048,256]{1,0:T(8,128)(2,1)} %convolution_convert_fusion.4.query_ref, bf16[2560,512]{1,0:T(8,128)(2,1)} %pad_maximum_fusion.pair_ref, s32[1,2048]{1,0:T(1,128)} %bitcast.33, s32[2560,1]{1,0:T(8,128)} %reshape.89.record_key_ref, ...), custom_call_target="tpu_custom_call" | custom-call | flops 6442450944 | bytes 4194304 | tf_op jit(solution)/shard_map/attention_forward/pallas_call | solution.py:178
  62.3 4.5 %collective-permute-done.2 = bf16[2048,512]{1,0:T(8,128)(2,1)} collective-permute-done((bf16[2048,512]{1,0:T(8,128)(2,1)}, bf16[2048,512]{1,0:T(8,128)(2,1)}, u32[]{:S(2)}, u32[]{:S(2)}) %collective-permute-start.2) | collective-permute-done | bytes 2097184 | tf_op jit(solution)/shard_map/ppermute | solution.py:246
  66.8 3.1 %fusion.19 = (f32[2048]{0:T(1024)S(1)}, f32[2048,512]{1,0:T(8,128)S(1)}) fusion(bf16[2048,512]{1,0:T(8,128)(2,1)} %collective-permute-done.2, bf16[2048,512]{1,0:T(8,128)(2,1)} %get-tuple-element.17, bf16[2048,512]{1,0:T(8,128)(2,1)S(1)} %copy-done.6), kind=kLoop, calls=%fused_computation.69 | loop fusion | flops 6289408 | bytes 10493952 | tf_op jit(solution)/shard_map/reduce_sum | solution.py:37
  70.9 2.5 %fusion.18 = f32[2048,1024]{1,0:T(8,128)S(1)} fusion(bf16[512,1024]{1,0:T(8,128)(2,1)S(1)} %copy-done, f32[2048,512]{1,0:T(8,128)S(1)} %get-tuple-element.34, f32[512]{0:T(512)S(1)} %copy-done.31, f32[2048]{0:T(1024)S(1)} %add_rsqrt_fusion, f32[2048]{0:T(1024)S(1)} %broadcast_multiply_fusion.2), kind=kOutput, calls=%fused_computation.68 | convolution fusion | flops 2151677952 | bytes 13649920 | tf_op jit(solution)/shard_map/dot_general | solution.py:401
  73.4 5.5 %multiply_convert_fusion.1 = bf16[2048,1024]{1,0:T(8,128)(2,1)S(1)} fusion(f32[2048,1024]{1,0:T(8,128)S(1)} %fusion.18, bf16[2048,512]{1,0:T(8,128)(2,1)S(1)} %copy-done.16, bf16[1024,512]{1,0:T(8,128)(2,1)S(1)} %copy-done.32), kind=kOutput, calls=%fused_computation.1 | convolution fusion | flops 2168455168 | bytes 15728640 | tf_op jit(solution)/shard_map/dot_general | solution.py:404
  78.9 2.5 %convolution_convert_fusion = bf16[2048,512]{1,0:T(8,128)(2,1)S(1)} fusion(bf16[2048,1024]{1,0:T(8,128)(2,1)S(1)} %multiply_convert_fusion.1, bf16[512,1024]{1,0:T(8,128)(2,1)S(1)} %copy-done), kind=kOutput, calls=%fused_computation.19 | convolution fusion | flops 2148532224 | bytes 7340032 | tf_op jit(solution)/shard_map/dot_general | solution.py:410
  81.6 3.6 %convolution_convert_fusion.5 = bf16[512,1024]{1,0:T(8,128)(2,1)} fusion(bf16[2048,1024]{1,0:T(8,128)(2,1)S(1)} %multiply_convert_fusion.1, f32[2048,512]{1,0:T(8,128)S(1)} %get-tuple-element.34, f32[512]{0:T(512)S(1)} %copy-done.31, f32[2048]{0:T(1024)S(1)} %add_rsqrt_fusion, f32[2048]{0:T(1024)S(1)} %broadcast_multiply_fusion.2), kind=kOutput, calls=%fused_computation.33 | convolution fusion | flops 2152202240 | bytes 9455616 | tf_op jit(solution)/shard_map/dot_general | solution.py:409
  85.1 3.5 %multiply_convert_fusion.5 = bf16[1024,512]{1,0:T(8,128)(2,1)} fusion(bf16[2048,512]{1,0:T(8,128)(2,1)S(1)} %copy-done.16, f32[2048,1024]{1,0:T(8,128)S(1)} %fusion.18), kind=kOutput, calls=%fused_computation.28 | convolution fusion | flops 2159017984 | bytes 11534336 | tf_op jit(solution)/shard_map/dot_general | solution.py:408
  88.6 4.2 %fusion.4 = (f32[2048]{0:T(1024)S(1)}, f32[2048]{0:T(1024)S(1)}) fusion(bf16[2048,512]{1,0:T(8,128)(2,1)} %collective-permute-done.3, bf16[2048,512]{1,0:T(8,128)(2,1)S(1)} %convolution_convert_fusion, f32[512]{0:T(512)S(1)} %copy-done.31, f32[2048]{0:T(1024)S(1)} %add_rsqrt_fusion, f32[2048,512]{1,0:T(8,128)} %copy-done.2, f32[2048]{0:T(1024)S(1)} %broadcast_multiply_fusion.2), kind=kLoop, calls=%fused_computation.18 | loop fusion | flops 9433088 | bytes 8423424 | tf_op jit(solution)/shard_map/reduce_sum | solution.py:45
  93.4 3.8 %multiply_add_fusion = f32[2048,512]{1,0:T(8,128)S(1)} fusion(bf16[2048,512]{1,0:T(8,128)(2,1)S(1)} %copy-done.17, f32[2048,512]{1,0:T(8,128)S(1)} %copy-done.3, bf16[2048,512]{1,0:T(8,128)(2,1)} %collective-permute-done.3, bf16[2048,512]{1,0:T(8,128)(2,1)S(1)} %convolution_convert_fusion, f32[2048]{0:T(1024)S(1)} %get-tuple-element.48, ...), kind=kLoop, calls=%fused_computation.10 | loop fusion | flops 12582912 | bytes 14714880 | tf_op jit(solution)/shard_map/add | solution.py:412
  97.2 1.7 convolution_convert_fusion.1.grad_ref
  99.9 29.2 %attention_backward.1 = (bf16[2048,256]{1,0:T(8,128)(2,1)}, bf16[2048,512]{1,0:T(8,128)(2,1)}, f32[512,512]{1,0:T(8,128)}, bf16[512,512]{1,0:T(8,128)(2,1)}) custom-call(bf16[2048,256]{1,0:T(8,128)(2,1)} %convolution_convert_fusion.4.query_ref, bf16[2560,512]{1,0:T(8,128)(2,1)} %pad_maximum_fusion.pair_ref, ...), custom_call_target="tpu_custom_call" | custom-call | flops 16106127360 | bytes 8388608 | tf_op jit(solution)/shard_map/attention_backward/pallas_call | solution.py:211
  130.4 3.5 %collective-permute-start.4 = (bf16[256,512]{1,0:T(8,128)(2,1)S(1)}, bf16[256,512]{1,0:T(8,128)(2,1)S(1)}, u32[]{:S(2)}, u32[]{:S(2)}) collective-permute-start(bf16[256,512]{1,0:T(8,128)(2,1)S(1)} %get-tuple-element.46), channel_id=1, source_target_pairs={{0,2},{2,4},{4,6},{6,8},{8,10},{10,12},{12,14},{14,16},{16,18},{18... | collective-permute-start | bytes 786440 | tf_op jit(solution)/shard_map/ppermute | solution.py:423
  135.2 1.5 slice.67
  136.8 1.5 fusion.6
  138.3 8.1 %collective-permute-done.4 = bf16[256,512]{1,0:T(8,128)(2,1)S(1)} collective-permute-done((bf16[256,512]{1,0:T(8,128)(2,1)S(1)}, bf16[256,512]{1,0:T(8,128)(2,1)S(1)}, u32[]{:S(2)}, u32[]{:S(2)}) %collective-permute-start.4) | collective-permute-done | bytes 262176 | tf_op jit(solution)/shard_map/ppermute | solution.py:423
  155.0 47.3 %slab_sum.1 = f32[4,4,128,256]{3,2,1,0:T(8,128)} custom-call(bf16[4,4,128,256]{3,2,1,0:T(8,128)(2,1)} %bitcast.1.x_ref), custom_call_target="tpu_custom_call" | custom-call | flops 2097152 | bytes 52428800 | tf_op jit(solution)/shard_map/slab_sum/pallas_call | solution.py:339
  204.3 20.1 %all-reduce.4.cloned.1.call-done = (bf16[512,1024]{1,0:T(8,128)(2,1)}, bf16[1024,512]{1,0:T(8,128)(2,1)}) async-done(((bf16[512,1024]{1,0:T(8,128)(2,1)}, bf16[1024,512]{1,0:T(8,128)(2,1)}), (bf16[512,1024]{1,0:T(8,128)(2,1)}, bf16[1024,512]{1,0:T(8,128)(2,1)})) %all-reduce.4.cloned.1.call-update) | async-done | bytes 2097168 | tf_op jit(solution)/shard_map/psum | solution.py:452
  224.4 2.7 %fusion.21 = (f32[1,4,128,256]{3,2,1,0:T(8,128)}, f32[1,4,128,256]{3,2,1,0:T(8,128)}, f32[1,4,128,256]{3,2,1,0:T(8,128)}) fusion(f32[4,4,128,256]{3,2,1,0:T(8,128)} %slab_sum.1), kind=kLoop, calls=%fused_computation.71 | loop fusion | bytes 3145728 | tf_op jit(solution)/shard_map/slice | solution.py:473
  227.1 2.8 %convert_multiply_fusion.1 = f32[512,1024]{1,0:T(8,128)} fusion(bf16[512,1024]{1,0:T(8,128)(2,1)} %get-tuple-element.25), kind=kLoop, calls=%fused_computation.27 | loop fusion | flops 1048576 | bytes 3145728 | tf_op jit(solution)/shard_map/mul | solution.py:475
  229.9 1.6 convert_multiply_fusion
  233.3 3.2 %multiply_add_fusion.1 = f32[1024,512]{1,0:T(8,128)} fusion(f32[2048,512]{1,0:T(8,128)S(1)} %copy-done.5, s32[]{:T(128)} %select_n.20, f32[2048,512]{1,0:T(8,128)S(1)} %copy-done.7, bf16[1024,512]{1,0:T(8,128)(2,1)} %copy-done.15, f32[1024]{0:T(1024)S(1)} %broadcast_multiply_fusion.4, f32[1024]{0:T(1024)S(1)} %broadcast_multiply_fusion.5, ...), kind=kLoop, calls=%fused_computation.29 | loop fusion | flops 4718592 | bytes 8402948 | tf_op jit(solution)/shard_map/add | solution.py:448
  (105 shorter events, 21.2 us)
Async XLA Ops:
  7.2 63.7 %copy-start = (bf16[512,1024]{1,0:T(8,128)(2,1)S(1)}, bf16[512,1024]{1,0:T(8,128)(2,1)}, u32[]{:S(2)}) copy-start(bf16[512,1024]{1,0:T(8,128)(2,1)} %param.20) | copy-start | bytes 3145732
  7.2 4.7 %copy-start.6 = (bf16[2048,512]{1,0:T(8,128)(2,1)S(1)}, bf16[2048,512]{1,0:T(8,128)(2,1)}, u32[]{:S(2)}) copy-start(bf16[2048,512]{1,0:T(8,128)(2,1)} %param.11) | copy-start | bytes 6291460
  7.2 4.7 %copy-start.30 = (f32[512]{0:T(512)S(1)}, f32[512]{0:T(512)}, u32[]{:S(2)}) copy-start(f32[512]{0:T(512)} %param.14) | copy-start | bytes 6148
  7.2 217.2 %all-reduce.4.cloned.1.call-start = ((), (), s32[]{:S(2)}) async-start(), calls=%async_computation | async-start | bytes 4194304 | tf_op jit(solution)/shard_map/psum | solution.py:452
  11.9 50.5 %copy-start.29 = (f32[2048]{0:T(1024)}, f32[2048]{0:T(1024)S(1)}, u32[]{:S(2)}) copy-start(f32[2048]{0:T(1024)S(1)} %add_rsqrt_fusion.1) | copy-start | bytes 24580
  15.4 8.9 %copy-start.21 = (s32[32768]{0:T(1024)S(1)}, s32[32768]{0:T(1024)}, u32[]{:S(2)}) copy-start(s32[32768]{0:T(1024)} %param.13) | copy-start | bytes 393220
  15.4 11.7 %copy-start.22 = (bf16[512,256]{1,0:T(8,128)(2,1)S(1)}, bf16[512,256]{1,0:T(8,128)(2,1)}, u32[]{:S(2)}) copy-start(bf16[512,256]{1,0:T(8,128)(2,1)} %param.15) | copy-start | bytes 786436
  17.3 16.4 %collective-permute-start = (bf16[256,512]{1,0:T(8,128)(2,1)}, bf16[256,512]{1,0:T(8,128)(2,1)}, u32[]{:S(2)}, u32[]{:S(2)}) collective-permute-start(bf16[256,512]{1,0:T(8,128)(2,1)} %get-tuple-element.42), channel_id=1, source_target_pairs={{0,2},{2,4},{4,6},{6,8},{8,10},{10,12},{12,14},{14,16},{16,18},{18... | collective-permute-start | bytes 786440 | tf_op jit(solution)/shard_map/ppermute | solution.py:27
  22.9 12.7 %collective-permute-start.1 = (bf16[256,512]{1,0:T(8,128)(2,1)}, bf16[256,512]{1,0:T(8,128)(2,1)}, u32[]{:S(2)}, u32[]{:S(2)}) collective-permute-start(bf16[256,512]{1,0:T(8,128)(2,1)} %get-tuple-element.43), channel_id=1, source_target_pairs={{2,0},{4,2},{6,4},{8,6},{10,8},{12,10},{14,12},{16,14},{18,16},{20... | collective-permute-start | bytes 786440 | tf_op jit(solution)/shard_map/ppermute | solution.py:29
  24.4 11.2 %copy-start.11 = (bf16[2048,256]{1,0:T(8,128)(2,1)S(1)}, bf16[2048,256]{1,0:T(8,128)(2,1)}, u32[]{:S(2)}) copy-start(bf16[2048,256]{1,0:T(8,128)(2,1)} %copy-done.10) | copy-start | bytes 3145732
  24.4 11.2 %copy-start.13 = (bf16[2048,256]{1,0:T(8,128)(2,1)S(1)}, bf16[2048,256]{1,0:T(8,128)(2,1)}, u32[]{:S(2)}) copy-start(bf16[2048,256]{1,0:T(8,128)(2,1)} %copy-done.12) | copy-start | bytes 3145732
  62.3 4.5 %collective-permute-start.2 = (bf16[2048,512]{1,0:T(8,128)(2,1)}, bf16[2048,512]{1,0:T(8,128)(2,1)}, u32[]{:S(2)}, u32[]{:S(2)}) collective-permute-start(bf16[2048,512]{1,0:T(8,128)(2,1)} %get-tuple-element.17), channel_id=1, source_target_pairs={{0,1},{1,0},{2,3},{3,2},{4,5},{5,4},{6,7},{7,6},{8,9},{9,8},{10,11... | collective-permute-start | bytes 6291464 | tf_op jit(solution)/shard_map/ppermute | solution.py:246
  69.9 11.6 %copy-start.2 = (f32[2048,512]{1,0:T(8,128)}, f32[2048,512]{1,0:T(8,128)S(1)}, u32[]{:S(2)}) copy-start(f32[2048,512]{1,0:T(8,128)S(1)} %get-tuple-element.34) | copy-start | bytes 12582916
  70.9 2.5 %copy-start.16 = (bf16[2048,512]{1,0:T(8,128)(2,1)S(1)}, bf16[2048,512]{1,0:T(8,128)(2,1)}, u32[]{:S(2)}) copy-start(bf16[2048,512]{1,0:T(8,128)(2,1)} %param.12) | copy-start | bytes 6291460
  70.9 2.5 %copy-start.32 = (bf16[1024,512]{1,0:T(8,128)(2,1)S(1)}, bf16[1024,512]{1,0:T(8,128)(2,1)}, u32[]{:S(2)}) copy-start(bf16[1024,512]{1,0:T(8,128)(2,1)} %param.21) | copy-start | bytes 3145732
  81.3 7.3 %collective-permute-start.3 = (bf16[2048,512]{1,0:T(8,128)(2,1)S(1)}, bf16[2048,512]{1,0:T(8,128)(2,1)}, u32[]{:S(2)}, u32[]{:S(2)}) collective-permute-start(bf16[2048,512]{1,0:T(8,128)(2,1)S(1)} %convolution_convert_fusion), channel_id=1, source_target_pairs={{0,1},{1,0},{2,3},{3,2},{4,5},{5,4},{6,7},{7,6},{8,9},{9,8},{10,11... | collective-permute-start | bytes 6291464 | tf_op jit(solution)/shard_map/ppermute | solution.py:246
  88.6 4.3 %copy-start.3 = (f32[2048,512]{1,0:T(8,128)S(1)}, f32[2048,512]{1,0:T(8,128)}, u32[]{:S(2)}) copy-start(f32[2048,512]{1,0:T(8,128)} %copy-done.2) | copy-start | bytes 12582916
  88.6 4.7 %copy-start.17 = (bf16[2048,512]{1,0:T(8,128)(2,1)S(1)}, bf16[2048,512]{1,0:T(8,128)(2,1)}, u32[]{:S(2)}) copy-start(bf16[2048,512]{1,0:T(8,128)(2,1)} %param.12) | copy-start | bytes 6291460
  93.4 3.8 %copy-start.24 = (bf16[256,512]{1,0:T(8,128)(2,1)S(1)}, bf16[256,512]{1,0:T(8,128)(2,1)}, u32[]{:S(2)}) copy-start(bf16[256,512]{1,0:T(8,128)(2,1)} %weight_ref.1) | copy-start | bytes 786436
  97.2 2.7 %copy-start.4 = (f32[2048,512]{1,0:T(8,128)}, f32[2048,512]{1,0:T(8,128)S(1)}, u32[]{:S(2)}) copy-start(f32[2048,512]{1,0:T(8,128)S(1)} %multiply_add_fusion) | copy-start | bytes 12582916
  129.1 7.6 %copy-start.9 = (bf16[2048,512]{1,0:T(8,128)(2,1)S(1)}, bf16[2048,512]{1,0:T(8,128)(2,1)}, u32[]{:S(2)}) copy-start(bf16[2048,512]{1,0:T(8,128)(2,1)} %copy-done.8) | copy-start | bytes 6291460
  129.1 7.6 %copy-start.14 = (bf16[2048,256]{1,0:T(8,128)(2,1)S(1)}, bf16[2048,256]{1,0:T(8,128)(2,1)}, u32[]{:S(2)}) copy-start(bf16[2048,256]{1,0:T(8,128)(2,1)} %get-tuple-element.19) | copy-start | bytes 3145732
  129.2 17.9 %copy-start.19 = (f32[512,512]{1,0:T(8,128)S(1)}, f32[512,512]{1,0:T(8,128)}, u32[]{:S(2)}) copy-start(f32[512,512]{1,0:T(8,128)} %get-tuple-element.20) | copy-start | bytes 3145732
  130.4 16.0 %collective-permute-start.4 = (bf16[256,512]{1,0:T(8,128)(2,1)S(1)}, bf16[256,512]{1,0:T(8,128)(2,1)S(1)}, u32[]{:S(2)}, u32[]{:S(2)}) collective-permute-start(bf16[256,512]{1,0:T(8,128)(2,1)S(1)} %get-tuple-element.46), channel_id=1, source_target_pairs={{0,2},{2,4},{4,6},{6,8},{8,10},{10,12},{12,14},{14,16},{16,18},{18... | collective-permute-start | bytes 786440 | tf_op jit(solution)/shard_map/ppermute | solution.py:423
  133.9 13.1 %collective-permute-start.5 = (bf16[256,512]{1,0:T(8,128)(2,1)S(1)}, bf16[256,512]{1,0:T(8,128)(2,1)S(1)}, u32[]{:S(2)}, u32[]{:S(2)}) collective-permute-start(bf16[256,512]{1,0:T(8,128)(2,1)S(1)} %get-tuple-element.47), channel_id=1, source_target_pairs={{2,0},{4,2},{6,4},{8,6},{10,8},{12,10},{14,12},{16,14},{18,16},{20... | collective-permute-start | bytes 786440 | tf_op jit(solution)/shard_map/ppermute | solution.py:424
  136.8 10.6 %copy-start.26 = (bf16[512,256]{1,0:T(8,128)(2,1)S(1)}, bf16[512,256]{1,0:T(8,128)(2,1)}, u32[]{:S(2)}) copy-start(bf16[512,256]{1,0:T(8,128)(2,1)} %param.17) | copy-start | bytes 786436
  150.8 80.8 %collective-permute-start.6 = (bf16[1024,512]{1,0:T(8,128)(2,1)}, bf16[1024,512]{1,0:T(8,128)(2,1)S(1)}, u32[]{:S(2)}, u32[]{:S(2)}) collective-permute-start(bf16[1024,512]{1,0:T(8,128)(2,1)} %constant_dynamic-slice_fusion), channel_id=1, source_target_pairs={{0,1},{1,0},{2,3},{3,2},{4,5},{5,4},{6,7},{7,6},{8,9},{9,8},{10,11... | collective-permute-start | bytes 3145736 | tf_op jit(solution)/shard_map/ppermute | solution.py:246
  224.4 5.5 %copy-start.18 = (bf16[1024,512]{1,0:T(8,128)(2,1)S(1)}, bf16[1024,512]{1,0:T(8,128)(2,1)}, u32[]{:S(2)}) copy-start(bf16[1024,512]{1,0:T(8,128)(2,1)} %get-tuple-element.26) | copy-start | bytes 3145732
  224.4 8.2 %copy-start.7 = (f32[2048,512]{1,0:T(8,128)S(1)}, f32[2048,512]{1,0:T(8,128)}, u32[]{:S(2)}) copy-start(f32[2048,512]{1,0:T(8,128)} %get-tuple-element.35) | copy-start | bytes 12582916
  229.9 3.4 %copy-start.5 = (f32[2048,512]{1,0:T(8,128)S(1)}, f32[2048,512]{1,0:T(8,128)}, u32[]{:S(2)}) copy-start(f32[2048,512]{1,0:T(8,128)} %copy-done.4) | copy-start | bytes 12582916
  229.9 3.4 %dynamic-slice-start = ((f32[2048]{0:T(1024)}, s32[]{:T(128)}), f32[1024]{0:T(1024)S(1)}, s32[]{:S(2)}) async-start(f32[2048]{0:T(1024)} %copy-done.29, s32[]{:T(128)} %select_n.20), calls=%async_computation.1 | async-start | bytes 8704 | tf_op jit(solution)/shard_map/dynamic-slice
  233.3 3.2 %copy-start.1 = (bf16[512,1024]{1,0:T(8,128)(2,1)S(1)}, bf16[512,1024]{1,0:T(8,128)(2,1)}, u32[]{:S(2)}) copy-start(bf16[512,1024]{1,0:T(8,128)(2,1)} %param.20) | copy-start | bytes 3145732
  (10 other events, 14.6 us)
Sparse Core Ops, SparseCore 0:
  88.7 135.6 all-reduce.3
